TPU v7x, 32 devices: a whole 2x2x4 slice. The times are simulated.
32 devices in a mesh: area: 8 (over z, x), row: 4 (over y, core).
Axes of the slice: x: 2, y: 2, z: 4, core: 2. Of those that a mesh axis runs over, the one named last changes fastest.
Arguments:
- conductance_inverse: float32 [32, 1024, 1024], P(('area', 'row')), as said below
- cap_history: float32 [32, 1024, 128], P(('area', 'row')), may hold values from -3 to 3
- cap_conductance: float32 [32, 1024], P(('area', 'row')), may hold values from 0.5 to 0.8
- wave_history: float32 [32, 40, 32, 128], P(('area', 'row')), may hold values from -6 to 6
- line_partner: int32 [32, 32], P(('area', 'row')), may hold values from 0 to 31, as said below
- line_node: int32 [32, 32], P(('area', 'row')), may hold values from 0 to 1023
- line_delay: int32 [32, 32], P(('area', 'row')), may hold values from 20 to 40
- line_admittance: float32 [32, 32], P(('area', 'row')), may hold values from 0.2 to 1
- conv_node: int32 [32, 64], P(('area', 'row')), may hold values from 0 to 1023
- conv_count: int32 [32], P(('area', 'row')), may hold values from 1 to 64, as said below
- conv_state: float32 [32, 2, 64, 128], P(('area', 'row')), may hold values from -3 to 3
- conv_reference: float32 [32, 2, 64, 128], P(('area', 'row')), may hold values from -4 to 4
- conv_rate: float32 [32, 64], P(('area', 'row')), may hold values from 0.03 to 0.6
- conv_limit: float32 [32, 64], P(('area', 'row')), may hold values from 1 to 2.5
- port_node: int32 [32, 8], P(('area', 'row')), may hold values from 0 to 1023
- port_admittance: float32 [32, 8], P(('area', 'row')), may hold values from 0.3 to 1.2
- port_voltage_prev: float32 [2, 32, 8, 128], P(None, ('area', 'row')), may hold values from -5 to 5
- port_bus: int32 [32, 8], P('area'), may hold values from 0 to 20479
- transfer_impedance: float32 [2, 20480, 256], P(None, 'row', 'area'), may hold values from -0.75 to 0.75
Outputs:
- waves: float32 [32, 20, 32, 128], P(('area', 'row'))
- cap_history_out: float32 [32, 1024, 128], P(('area', 'row'))
- conv_state_out: float32 [32, 2, 64, 128], P(('area', 'row'))
- bus_voltage: float32 [2, 20480, 128], P(None, 'row')
- port_voltage: float32 [2, 32, 8, 128], P(None, ('area', 'row'))
Inputs may be any that keep to these rules, and one draw needn't show every extreme that they name: Slot l < 16 of subnetwork s and slot l + 16 of subnetwork (s + k_l) mod 32 are the two ends of one line, with k_l in 1 or 2 the same for every subnetwork and exactly 12 of the k_l equal to 1; so line_partner[s, l] = (s + k_l) mod 32 and line_partner[s, l + 16] = (s - k_l) mod 32. `conv_count`: some subnetwork has all 64 converters in service. `conductance_inverse`: each subnetwork's inverse nodal conductance matrix.
All inputs are finite; a program needn't handle non-finite values.
Results may differ from a plain program's by a relative error of at most 0.0003.
Values sent between devices are 32-bit elements; how exact they have to be, the bound alone decides.
A program may use at most 64 MiB of HBM per device.

v0:
```python
import math

import jax
import jax.numpy as jnp
from jax import lax
from jax.sharding import PartitionSpec as P

STEPS = 20
HIST = 40
NEAR = 12


HIGHEST = lax.Precision.HIGHEST
SAG_FACTOR = 0.3


def from_behind(x, axis, by):
    size = lax.axis_size(axis)
    return lax.ppermute(x, axis, [(i, (i + by) % size) for i in range(size)])


def window(
    ginv,
    start_hist,
    gcap,
    incoming,
    lnode,
    ladm,
    cnode,
    ccount,
    cstate,
    setpoint_flow,
    crate,
    climit,
    pnode,
    padm,
    pvolt,
):
    nodes = ginv.shape[0]
    lines = lnode.shape[0]
    convs = cnode.shape[0]
    index = jnp.concatenate([lnode, cnode, pnode])
    onehot = (jnp.arange(nodes, dtype=jnp.int32)[:, None] == index[None, :]).astype(jnp.float32)
    picker = onehot.T
    live = (jnp.arange(convs, dtype=jnp.int32) < ccount)[:, None]
    angles = jnp.arange(1, STEPS + 1, dtype=jnp.float32) * jnp.float32(2.0 * math.pi / STEPS)
    limit = climit[:, None]
    slew_limit = crate[:, None]

    def advance(carry, inputs):
        hist_now, inverter_axial_part, inverter_normal_part, acc_re, acc_im = carry
        inward, angle = inputs
        angle_cos_factor = jnp.cos(angle)
        angle_sin_factor = jnp.sin(angle)
        drive = jnp.where(
            live,
            inverter_axial_part * angle_cos_factor - inverter_normal_part * angle_sin_factor,
            0.0,
        )
        source = padm[:, None] * (pvolt[0] * angle_cos_factor - pvolt[1] * angle_sin_factor)
        stacked = jnp.concatenate([inward, drive, source], axis=0)
        right = hist_now + jnp.dot(onehot, stacked, precision=HIGHEST)
        volt = jnp.dot(ginv, right, precision=HIGHEST)
        probe = jnp.dot(picker, volt, precision=HIGHEST)
        at_line = probe[:lines]
        inverter_emf = probe[lines : lines + convs]
        at_port = probe[lines + convs :]
        outward = 2.0 * ladm[:, None] * at_line - inward
        flow = source - padm[:, None] * at_port
        acc_re = acc_re + flow * angle_cos_factor
        acc_im = acc_im - flow * angle_sin_factor
        unclipped_axial_part = (
            inverter_axial_part
            + slew_limit * (setpoint_flow[0] - inverter_axial_part)
            - SAG_FACTOR * inverter_emf * angle_cos_factor
        )
        unclipped_normal_part = (
            inverter_normal_part
            + slew_limit * (setpoint_flow[1] - inverter_normal_part)
            + SAG_FACTOR * inverter_emf * angle_sin_factor
        )
        inverter_axial_part = jnp.where(
            live, limit * jnp.tanh(unclipped_axial_part / limit), inverter_axial_part
        )
        inverter_normal_part = jnp.where(
            live, limit * jnp.tanh(unclipped_normal_part / limit), inverter_normal_part
        )
        hist_now = 2.0 * gcap[:, None] * volt - hist_now
        return ((hist_now, inverter_axial_part, inverter_normal_part, acc_re, acc_im), outward)

    zeros = jnp.zeros(pvolt.shape[1:], dtype=jnp.float32)
    carry = (start_hist, cstate[0], cstate[1], zeros, zeros)
    carry, outward = lax.scan(advance, carry, (incoming, angles))
    hist_end, inverter_axial_part, inverter_normal_part, acc_re, acc_im = carry
    current = jnp.stack([acc_re, acc_im]) * jnp.float32(2.0 / STEPS)
    return (outward, hist_end, jnp.stack([inverter_axial_part, inverter_normal_part]), current)


def per_device(
    conductance_inverse,
    cap_history,
    cap_conductance,
    wave_history,
    line_partner,
    line_node,
    line_delay,
    line_admittance,
    conv_node,
    conv_count,
    conv_state,
    conv_reference,
    conv_rate,
    conv_limit,
    port_node,
    port_admittance,
    port_voltage_prev,
    port_bus,
    transfer_impedance,
):
    subnets = lax.axis_size(("area", "row"))
    own = lax.axis_index(("area", "row"))
    history = wave_history[0]
    lines = history.shape[1]
    partner = line_partner[0]
    offset = (partner - own) % subnets
    signed = jnp.where(offset > subnets // 2, offset - subnets, offset)
    remote = (jnp.arange(lines, dtype=jnp.int32) + lines // 2) % lines
    combined = jnp.zeros(history.shape, jnp.float32)
    for reach in (1, -1, 2, -2):
        count = NEAR if abs(reach) == 1 else lines // 2 - NEAR
        sending = signed == reach
        order = jnp.argsort(jnp.where(sending, 0, 1), stable=True)[:count]
        packed = jnp.take(history, order, axis=1)
        arrived = from_behind(packed, ("area", "row"), reach)
        rank = jnp.cumsum(sending.astype(jnp.int32)) - 1
        slot = jnp.clip(rank[remote], 0, count - 1)
        picked = jnp.take(arrived, slot, axis=1)
        combined = combined + jnp.where((signed == -reach)[None, :, None], picked, 0.0)
    delay = line_delay[0]
    where_now = jnp.arange(STEPS, dtype=jnp.int32)[:, None] - delay[None, :] + HIST
    select = (where_now[:, None, :] == jnp.arange(HIST, dtype=jnp.int32)[None, :, None]).astype(
        jnp.float32
    )
    incoming = jnp.einsum("thl,hlc->tlc", select, combined, precision=HIGHEST)
    outward, hist_end, conv_out, current = window(
        conductance_inverse[0],
        cap_history[0],
        cap_conductance[0],
        incoming,
        line_node[0],
        line_admittance[0],
        conv_node[0],
        conv_count[0],
        conv_state[0],
        conv_reference[0],
        conv_rate[0],
        conv_limit[0],
        port_node[0],
        port_admittance[0],
        port_voltage_prev[:, 0],
    )
    bus_rows = transfer_impedance.shape[1]
    cases = current.shape[2]
    piece = lax.all_gather(current[:, None], "row", axis=1, tiled=True)
    members = piece.shape[1]
    ports = piece.shape[2]
    flat = piece.reshape(2, members * ports, cases)
    real = jnp.dot(transfer_impedance[0], flat[0], precision=HIGHEST) - jnp.dot(
        transfer_impedance[1], flat[1], precision=HIGHEST
    )
    imag = jnp.dot(transfer_impedance[0], flat[1], precision=HIGHEST) + jnp.dot(
        transfer_impedance[1], flat[0], precision=HIGHEST
    )
    partial_bus = jnp.stack([real, imag])
    bus_voltage = lax.psum(partial_bus, "area")
    first_row = lax.axis_index("row") * bus_rows
    local_bus = (port_bus - first_row).reshape(-1)
    pick_rows = (local_bus[:, None] == jnp.arange(bus_rows, dtype=jnp.int32)[None, :]).astype(
        jnp.float32
    )
    gathered = jnp.einsum("jb,xbc->xjc", pick_rows, bus_voltage, precision=HIGHEST)
    gathered = gathered.reshape(2, port_bus.shape[0], port_bus.shape[1], cases)
    port_voltage = lax.psum_scatter(gathered, "row", scatter_dimension=1, tiled=True)
    return (outward[None], hist_end[None], conv_out[None], bus_voltage, port_voltage)


def solution(mesh):
    placed = (
        P(("area", "row"), None, None),
        P(("area", "row"), None, None),
        P(("area", "row"), None),
        P(("area", "row"), None, None, None),
        P(("area", "row"), None),
        P(("area", "row"), None),
        P(("area", "row"), None),
        P(("area", "row"), None),
        P(("area", "row"), None),
        P(("area", "row")),
        P(("area", "row"), None, None, None),
        P(("area", "row"), None, None, None),
        P(("area", "row"), None),
        P(("area", "row"), None),
        P(("area", "row"), None),
        P(("area", "row"), None),
        P(None, ("area", "row"), None, None),
        P("area", None),
        P(None, "row", "area"),
    )
    return jax.shard_map(
        per_device,
        mesh=mesh,
        in_specs=placed,
        out_specs=(
            P(("area", "row"), None, None, None),
            P(("area", "row"), None, None),
            P(("area", "row"), None, None, None),
            P(None, "row", None),
            P(None, ("area", "row"), None, None),
        ),
        check_vma=False,
    )
```

profile of v0, /device:TPU:20, one launch (start us, length us, event | category | flops | bytes accessed | tf_op | source)
XLA Modules:
  0.0 519.3 jit_solution(1617881758800676381)
XLA Ops:
  7.9 1.6 sort.61
  9.6 1.5 copy.56
  11.7 1.4 collective-permute-start.2
  13.1 1.6 sort.62
  16.0 1.6 sort.60
  18.3 1.2 collective-permute-start.1
  19.5 1.6 sort.59
  22.6 0.7 gather_fusion
  25.1 0.7 gather_fusion.3
  28.2 1.4 gather_fusion.7
  29.6 2.7 convolution_bitcast_fusion.2
  32.4 254.0 %while.23 = (s32[]{:T(128)}, f32[1024,128]{0,1:T(8,128)S(1)}, f32[64,128]{1,0:T(8,128)S(1)}, f32[64,128]{1,0:T(8,128)S(1)}, f32[8,128]{1,0:T(8,128)S(1)}, /*inde...) while((s32[]{:T(128)}, f32[1024,128]{0,1:T(8,128)S(1)}, ...), condition=%wide.region_9.14_spmd.clone.clone.clone, body=%wide.region_8.13_spmd.clone.clone.clone.sunk | while | flops 1938803712 | bytes 8437999 | solution.py:93
  35.2 0.9 constant_dynamic-slice_fusion.3
  36.8 6.7 %bitcast_subtract_fusion.4 = (f32[1024,128]{0,1:T(8,128)S(1)}, f32[128,1024]{1,0:T(8,128)S(1)}) fusion(f32[1024,128]{0,1:T(8,128)S(1)} %get-tuple-element.591, f32[1024]{0:T(1024)S(1)} %bitcast.217, f32[1024,128]{0,1:T(8,128)S(1)} %fusion.99, f32[1024,1024]{1,0:T(8,128)} %get-tuple-element.624), kind=kOutput, calls=%fused_computation.18.clone.1 | convolution fusion | flops 1610874880 | bytes 6295552 | tf_op jit(solution)/shard_map/while/body/eval_jaxpr/dot_general | solution.py:63
  47.9 0.9 constant_dynamic-slice_fusion.3
  49.5 6.7 %bitcast_subtract_fusion.4 = (f32[1024,128]{0,1:T(8,128)S(1)}, f32[128,1024]{1,0:T(8,128)S(1)}) fusion(f32[1024,128]{0,1:T(8,128)S(1)} %get-tuple-element.591, f32[1024]{0:T(1024)S(1)} %bitcast.217, f32[1024,128]{0,1:T(8,128)S(1)} %fusion.99, f32[1024,1024]{1,0:T(8,128)} %get-tuple-element.624), kind=kOutput, calls=%fused_computation.18.clone.1 | convolution fusion | flops 1610874880 | bytes 6295552 | tf_op jit(solution)/shard_map/while/body/eval_jaxpr/dot_general | solution.py:63
  60.6 0.9 constant_dynamic-slice_fusion.3
  62.2 6.7 %bitcast_subtract_fusion.4 = (f32[1024,128]{0,1:T(8,128)S(1)}, f32[128,1024]{1,0:T(8,128)S(1)}) fusion(f32[1024,128]{0,1:T(8,128)S(1)} %get-tuple-element.591, f32[1024]{0:T(1024)S(1)} %bitcast.217, f32[1024,128]{0,1:T(8,128)S(1)} %fusion.99, f32[1024,1024]{1,0:T(8,128)} %get-tuple-element.624), kind=kOutput, calls=%fused_computation.18.clone.1 | convolution fusion | flops 1610874880 | bytes 6295552 | tf_op jit(solution)/shard_map/while/body/eval_jaxpr/dot_general | solution.py:63
  73.3 0.9 constant_dynamic-slice_fusion.3
  74.9 6.7 %bitcast_subtract_fusion.4 = (f32[1024,128]{0,1:T(8,128)S(1)}, f32[128,1024]{1,0:T(8,128)S(1)}) fusion(f32[1024,128]{0,1:T(8,128)S(1)} %get-tuple-element.591, f32[1024]{0:T(1024)S(1)} %bitcast.217, f32[1024,128]{0,1:T(8,128)S(1)} %fusion.99, f32[1024,1024]{1,0:T(8,128)} %get-tuple-element.624), kind=kOutput, calls=%fused_computation.18.clone.1 | convolution fusion | flops 1610874880 | bytes 6295552 | tf_op jit(solution)/shard_map/while/body/eval_jaxpr/dot_general | solution.py:63
  86.0 0.9 constant_dynamic-slice_fusion.3
  87.6 6.7 %bitcast_subtract_fusion.4 = (f32[1024,128]{0,1:T(8,128)S(1)}, f32[128,1024]{1,0:T(8,128)S(1)}) fusion(f32[1024,128]{0,1:T(8,128)S(1)} %get-tuple-element.591, f32[1024]{0:T(1024)S(1)} %bitcast.217, f32[1024,128]{0,1:T(8,128)S(1)} %fusion.99, f32[1024,1024]{1,0:T(8,128)} %get-tuple-element.624), kind=kOutput, calls=%fused_computation.18.clone.1 | convolution fusion | flops 1610874880 | bytes 6295552 | tf_op jit(solution)/shard_map/while/body/eval_jaxpr/dot_general | solution.py:63
  98.7 0.9 constant_dynamic-slice_fusion.3
  100.3 6.7 %bitcast_subtract_fusion.4 = (f32[1024,128]{0,1:T(8,128)S(1)}, f32[128,1024]{1,0:T(8,128)S(1)}) fusion(f32[1024,128]{0,1:T(8,128)S(1)} %get-tuple-element.591, f32[1024]{0:T(1024)S(1)} %bitcast.217, f32[1024,128]{0,1:T(8,128)S(1)} %fusion.99, f32[1024,1024]{1,0:T(8,128)} %get-tuple-element.624), kind=kOutput, calls=%fused_computation.18.clone.1 | convolution fusion | flops 1610874880 | bytes 6295552 | tf_op jit(solution)/shard_map/while/body/eval_jaxpr/dot_general | solution.py:63
  111.4 0.9 constant_dynamic-slice_fusion.3
  113.0 6.7 %bitcast_subtract_fusion.4 = (f32[1024,128]{0,1:T(8,128)S(1)}, f32[128,1024]{1,0:T(8,128)S(1)}) fusion(f32[1024,128]{0,1:T(8,128)S(1)} %get-tuple-element.591, f32[1024]{0:T(1024)S(1)} %bitcast.217, f32[1024,128]{0,1:T(8,128)S(1)} %fusion.99, f32[1024,1024]{1,0:T(8,128)} %get-tuple-element.624), kind=kOutput, calls=%fused_computation.18.clone.1 | convolution fusion | flops 1610874880 | bytes 6295552 | tf_op jit(solution)/shard_map/while/body/eval_jaxpr/dot_general | solution.py:63
  124.1 0.9 constant_dynamic-slice_fusion.3
  125.7 6.7 %bitcast_subtract_fusion.4 = (f32[1024,128]{0,1:T(8,128)S(1)}, f32[128,1024]{1,0:T(8,128)S(1)}) fusion(f32[1024,128]{0,1:T(8,128)S(1)} %get-tuple-element.591, f32[1024]{0:T(1024)S(1)} %bitcast.217, f32[1024,128]{0,1:T(8,128)S(1)} %fusion.99, f32[1024,1024]{1,0:T(8,128)} %get-tuple-element.624), kind=kOutput, calls=%fused_computation.18.clone.1 | convolution fusion | flops 1610874880 | bytes 6295552 | tf_op jit(solution)/shard_map/while/body/eval_jaxpr/dot_general | solution.py:63
  136.8 0.9 constant_dynamic-slice_fusion.3
  138.4 6.7 %bitcast_subtract_fusion.4 = (f32[1024,128]{0,1:T(8,128)S(1)}, f32[128,1024]{1,0:T(8,128)S(1)}) fusion(f32[1024,128]{0,1:T(8,128)S(1)} %get-tuple-element.591, f32[1024]{0:T(1024)S(1)} %bitcast.217, f32[1024,128]{0,1:T(8,128)S(1)} %fusion.99, f32[1024,1024]{1,0:T(8,128)} %get-tuple-element.624), kind=kOutput, calls=%fused_computation.18.clone.1 | convolution fusion | flops 1610874880 | bytes 6295552 | tf_op jit(solution)/shard_map/while/body/eval_jaxpr/dot_general | solution.py:63
  149.5 0.9 constant_dynamic-slice_fusion.3
  151.1 6.7 %bitcast_subtract_fusion.4 = (f32[1024,128]{0,1:T(8,128)S(1)}, f32[128,1024]{1,0:T(8,128)S(1)}) fusion(f32[1024,128]{0,1:T(8,128)S(1)} %get-tuple-element.591, f32[1024]{0:T(1024)S(1)} %bitcast.217, f32[1024,128]{0,1:T(8,128)S(1)} %fusion.99, f32[1024,1024]{1,0:T(8,128)} %get-tuple-element.624), kind=kOutput, calls=%fused_computation.18.clone.1 | convolution fusion | flops 1610874880 | bytes 6295552 | tf_op jit(solution)/shard_map/while/body/eval_jaxpr/dot_general | solution.py:63
  162.2 0.9 constant_dynamic-slice_fusion.3
  163.8 6.7 %bitcast_subtract_fusion.4 = (f32[1024,128]{0,1:T(8,128)S(1)}, f32[128,1024]{1,0:T(8,128)S(1)}) fusion(f32[1024,128]{0,1:T(8,128)S(1)} %get-tuple-element.591, f32[1024]{0:T(1024)S(1)} %bitcast.217, f32[1024,128]{0,1:T(8,128)S(1)} %fusion.99, f32[1024,1024]{1,0:T(8,128)} %get-tuple-element.624), kind=kOutput, calls=%fused_computation.18.clone.1 | convolution fusion | flops 1610874880 | bytes 6295552 | tf_op jit(solution)/shard_map/while/body/eval_jaxpr/dot_general | solution.py:63
  174.9 0.9 constant_dynamic-slice_fusion.3
  176.5 6.7 %bitcast_subtract_fusion.4 = (f32[1024,128]{0,1:T(8,128)S(1)}, f32[128,1024]{1,0:T(8,128)S(1)}) fusion(f32[1024,128]{0,1:T(8,128)S(1)} %get-tuple-element.591, f32[1024]{0:T(1024)S(1)} %bitcast.217, f32[1024,128]{0,1:T(8,128)S(1)} %fusion.99, f32[1024,1024]{1,0:T(8,128)} %get-tuple-element.624), kind=kOutput, calls=%fused_computation.18.clone.1 | convolution fusion | flops 1610874880 | bytes 6295552 | tf_op jit(solution)/shard_map/while/body/eval_jaxpr/dot_general | solution.py:63
  187.6 0.9 constant_dynamic-slice_fusion.3
  189.2 6.7 %bitcast_subtract_fusion.4 = (f32[1024,128]{0,1:T(8,128)S(1)}, f32[128,1024]{1,0:T(8,128)S(1)}) fusion(f32[1024,128]{0,1:T(8,128)S(1)} %get-tuple-element.591, f32[1024]{0:T(1024)S(1)} %bitcast.217, f32[1024,128]{0,1:T(8,128)S(1)} %fusion.99, f32[1024,1024]{1,0:T(8,128)} %get-tuple-element.624), kind=kOutput, calls=%fused_computation.18.clone.1 | convolution fusion | flops 1610874880 | bytes 6295552 | tf_op jit(solution)/shard_map/while/body/eval_jaxpr/dot_general | solution.py:63
  200.3 0.9 constant_dynamic-slice_fusion.3
  201.9 6.7 %bitcast_subtract_fusion.4 = (f32[1024,128]{0,1:T(8,128)S(1)}, f32[128,1024]{1,0:T(8,128)S(1)}) fusion(f32[1024,128]{0,1:T(8,128)S(1)} %get-tuple-element.591, f32[1024]{0:T(1024)S(1)} %bitcast.217, f32[1024,128]{0,1:T(8,128)S(1)} %fusion.99, f32[1024,1024]{1,0:T(8,128)} %get-tuple-element.624), kind=kOutput, calls=%fused_computation.18.clone.1 | convolution fusion | flops 1610874880 | bytes 6295552 | tf_op jit(solution)/shard_map/while/body/eval_jaxpr/dot_general | solution.py:63
  213.0 0.9 constant_dynamic-slice_fusion.3
  214.6 6.7 %bitcast_subtract_fusion.4 = (f32[1024,128]{0,1:T(8,128)S(1)}, f32[128,1024]{1,0:T(8,128)S(1)}) fusion(f32[1024,128]{0,1:T(8,128)S(1)} %get-tuple-element.591, f32[1024]{0:T(1024)S(1)} %bitcast.217, f32[1024,128]{0,1:T(8,128)S(1)} %fusion.99, f32[1024,1024]{1,0:T(8,128)} %get-tuple-element.624), kind=kOutput, calls=%fused_computation.18.clone.1 | convolution fusion | flops 1610874880 | bytes 6295552 | tf_op jit(solution)/shard_map/while/body/eval_jaxpr/dot_general | solution.py:63
  225.7 0.9 constant_dynamic-slice_fusion.3
  227.3 6.7 %bitcast_subtract_fusion.4 = (f32[1024,128]{0,1:T(8,128)S(1)}, f32[128,1024]{1,0:T(8,128)S(1)}) fusion(f32[1024,128]{0,1:T(8,128)S(1)} %get-tuple-element.591, f32[1024]{0:T(1024)S(1)} %bitcast.217, f32[1024,128]{0,1:T(8,128)S(1)} %fusion.99, f32[1024,1024]{1,0:T(8,128)} %get-tuple-element.624), kind=kOutput, calls=%fused_computation.18.clone.1 | convolution fusion | flops 1610874880 | bytes 6295552 | tf_op jit(solution)/shard_map/while/body/eval_jaxpr/dot_general | solution.py:63
  238.4 0.9 constant_dynamic-slice_fusion.3
  240.0 6.7 %bitcast_subtract_fusion.4 = (f32[1024,128]{0,1:T(8,128)S(1)}, f32[128,1024]{1,0:T(8,128)S(1)}) fusion(f32[1024,128]{0,1:T(8,128)S(1)} %get-tuple-element.591, f32[1024]{0:T(1024)S(1)} %bitcast.217, f32[1024,128]{0,1:T(8,128)S(1)} %fusion.99, f32[1024,1024]{1,0:T(8,128)} %get-tuple-element.624), kind=kOutput, calls=%fused_computation.18.clone.1 | convolution fusion | flops 1610874880 | bytes 6295552 | tf_op jit(solution)/shard_map/while/body/eval_jaxpr/dot_general | solution.py:63
  251.1 0.9 constant_dynamic-slice_fusion.3
  252.7 6.7 %bitcast_subtract_fusion.4 = (f32[1024,128]{0,1:T(8,128)S(1)}, f32[128,1024]{1,0:T(8,128)S(1)}) fusion(f32[1024,128]{0,1:T(8,128)S(1)} %get-tuple-element.591, f32[1024]{0:T(1024)S(1)} %bitcast.217, f32[1024,128]{0,1:T(8,128)S(1)} %fusion.99, f32[1024,1024]{1,0:T(8,128)} %get-tuple-element.624), kind=kOutput, calls=%fused_computation.18.clone.1 | convolution fusion | flops 1610874880 | bytes 6295552 | tf_op jit(solution)/shard_map/while/body/eval_jaxpr/dot_general | solution.py:63
  263.8 0.9 constant_dynamic-slice_fusion.3
  265.4 6.7 %bitcast_subtract_fusion.4 = (f32[1024,128]{0,1:T(8,128)S(1)}, f32[128,1024]{1,0:T(8,128)S(1)}) fusion(f32[1024,128]{0,1:T(8,128)S(1)} %get-tuple-element.591, f32[1024]{0:T(1024)S(1)} %bitcast.217, f32[1024,128]{0,1:T(8,128)S(1)} %fusion.99, f32[1024,1024]{1,0:T(8,128)} %get-tuple-element.624), kind=kOutput, calls=%fused_computation.18.clone.1 | convolution fusion | flops 1610874880 | bytes 6295552 | tf_op jit(solution)/shard_map/while/body/eval_jaxpr/dot_general | solution.py:63
  276.5 0.9 constant_dynamic-slice_fusion.3
  278.1 6.7 %bitcast_subtract_fusion.4 = (f32[1024,128]{0,1:T(8,128)S(1)}, f32[128,1024]{1,0:T(8,128)S(1)}) fusion(f32[1024,128]{0,1:T(8,128)S(1)} %get-tuple-element.591, f32[1024]{0:T(1024)S(1)} %bitcast.217, f32[1024,128]{0,1:T(8,128)S(1)} %fusion.99, f32[1024,1024]{1,0:T(8,128)} %get-tuple-element.624), kind=kOutput, calls=%fused_computation.18.clone.1 | convolution fusion | flops 1610874880 | bytes 6295552 | tf_op jit(solution)/shard_map/while/body/eval_jaxpr/dot_general | solution.py:63
  286.4 6.4 %all_gather.3 = f32[2,4,8,128]{3,2,1,0:T(8,128)S(1)} all-gather(f32[2,1,8,128]{3,2,1,0:T(8,128)S(1)} %maximum_multiply_fusion), channel_id=1, replica_groups=mesh['area'=8,'row'=4] {'row'}, dimensions={1}, use_global_device_ids=true | all-gather | bytes 40960 | tf_op jit(solution)/shard_map/all_gather | solution.py:164
  292.8 2.2 fusion.39
  295.0 2.2 fusion.41
  297.3 2.3 fusion.36
  299.5 2.3 fusion.35
  301.8 2.9 pad_maximum_fusion
  306.1 1.0 copy.48
  307.8 182.0 %all-reduce.3.cloned.1.call-done = f32[2,5120,128]{1,2,0:T(8,128)} async-done(((f32[2,5120,128]{1,2,0:T(8,128)}), f32[2,5120,128]{1,2,0:T(8,128)}) %all-reduce.3.cloned.1.call-update) | async-done | bytes 5242896 | tf_op jit(solution)/shard_map/psum | solution.py:175
  489.8 5.2 convolution_bitcast_fusion.3
  495.0 10.4 %all-reduce = f32[2,4,8,128]{3,2,1,0:T(8,128)S(1)} all-reduce(f32[2,4,8,128]{3,2,1,0:T(8,128)S(1)} %convolution_bitcast_fusion.3), channel_id=2, replica_groups=mesh['area'=8,'row'=4] {'row'}, use_global_device_ids=true, to_apply=%region_11.16.clone | all-reduce | flops 8192 | bytes 65536
  505.4 1.2 constant_dynamic-slice_fusion.1
  506.6 5.9 %copy.50 = f32[2,5120,128]{2,1,0:T(8,128)} copy(f32[2,5120,128]{1,2,0:T(8,128)} %all-reduce.3.cloned.1.call-done) | data formatting | bytes 10485760
  (322 shorter events, 81.9 us)
Async XLA Ops:
  7.2 14.7 %copy-start.11 = (s32[1,32]{1,0:T(1,128)S(1)}, s32[1,32]{1,0:T(1,128)}, u32[]{:S(2)}) copy-start(s32[1,32]{1,0:T(1,128)} %param.33) | copy-start | bytes 388
  7.2 15.0 %copy-start.10 = (s32[1,32]{1,0:T(1,128)S(1)}, s32[1,32]{1,0:T(1,128)}, u32[]{:S(2)}) copy-start(s32[1,32]{1,0:T(1,128)} %param.35) | copy-start | bytes 388
  7.2 482.6 %all-reduce.3.cloned.1.call-start = ((), (), s32[]{:S(2)}) async-start(), calls=%async_computation | async-start | bytes 10485760 | tf_op jit(solution)/shard_map/psum | solution.py:175
  11.6 14.2 %copy-start.5 = (f32[1,2,64,128]{3,2,1,0:T(8,128)S(1)}, f32[1,2,64,128]{3,2,1,0:T(8,128)}, u32[]{:S(2)}) copy-start(f32[1,2,64,128]{3,2,1,0:T(8,128)} %param.39) | copy-start | bytes 196612
  11.7 15.2 %collective-permute-start.2 = (f32[40,4,128]{2,0,1:T(8,128)S(1)}, f32[40,4,128]{2,0,1:T(8,128)S(1)}, u32[]{:S(2)}, u32[]{:S(2)}) collective-permute-start(f32[40,4,128]{2,0,1:T(8,128)S(1)} %select_bitcast_fusion.3), channel_id=1, source_target_pairs={{0,2},{1,3},{2,4},{3,5},{4,6},{5,7},{6,8},{7,9},{8,10},{9,11},{10,... | collective-permute-start | bytes 245768 | tf_op jit(solution)/shard_map/ppermute | solution.py:19
  14.7 11.2 %copy-start.3 = (f32[1,1024,128]{2,1,0:T(8,128)S(1)}, f32[1,1024,128]{2,1,0:T(8,128)}, u32[]{:S(2)}) copy-start(f32[1,1024,128]{2,1,0:T(8,128)} %param.30) | copy-start | bytes 1572868
  15.4 10.8 %collective-permute-start.3 = (f32[40,4,128]{2,0,1:T(8,128)S(1)}, f32[40,4,128]{2,0,1:T(8,128)S(1)}, u32[]{:S(2)}, u32[]{:S(2)}) collective-permute-start(f32[40,4,128]{2,0,1:T(8,128)S(1)} %select_bitcast_fusion.2), channel_id=1, source_target_pairs={{0,30},{1,31},{2,0},{3,1},{4,2},{5,3},{6,4},{7,5},{8,6},{9,7},{10,... | collective-permute-start | bytes 245768 | tf_op jit(solution)/shard_map/ppermute | solution.py:19
  18.2 7.9 %copy-start.12 = (s32[1,8]{1,0:T(1,128)S(1)}, s32[1,8]{1,0:T(1,128)}, u32[]{:S(2)}) copy-start(s32[1,8]{1,0:T(1,128)} %param.43) | copy-start | bytes 100
  18.2 7.9 %copy-start.13 = (s32[1,64]{1,0:T(1,128)S(1)}, s32[1,64]{1,0:T(1,128)}, u32[]{:S(2)}) copy-start(s32[1,64]{1,0:T(1,128)} %param.37) | copy-start | bytes 772
  18.2 7.9 %copy-start.14 = (s32[1,32]{1,0:T(1,128)S(1)}, s32[1,32]{1,0:T(1,128)}, u32[]{:S(2)}) copy-start(s32[1,32]{1,0:T(1,128)} %param.34) | copy-start | bytes 388
  18.3 9.9 %collective-permute-start.1 = (f32[40,12,128]{2,0,1:T(8,128)S(1)}, f32[40,12,128]{2,0,1:T(8,128)S(1)}, u32[]{:S(2)}, u32[]{:S(2)}) collective-permute-start(f32[40,12,128]{2,0,1:T(8,128)S(1)} %select_bitcast_fusion), channel_id=1, source_target_pairs={{0,31},{1,0},{2,1},{3,2},{4,3},{5,4},{6,5},{7,6},{8,7},{9,8},{10,9... | collective-permute-start | bytes 737288 | tf_op jit(solution)/shard_map/ppermute | solution.py:19
  21.8 5.7 %collective-permute-start = (f32[40,12,128]{2,0,1:T(8,128)S(1)}, f32[40,12,128]{2,0,1:T(8,128)S(1)}, u32[]{:S(2)}, u32[]{:S(2)}) collective-permute-start(f32[40,12,128]{2,0,1:T(8,128)S(1)} %select_bitcast_fusion.1), channel_id=1, source_target_pairs={{0,1},{1,2},{2,3},{3,4},{4,5},{5,6},{6,7},{7,8},{8,9},{9,10},{10,1... | collective-permute-start | bytes 737288 | tf_op jit(solution)/shard_map/ppermute | solution.py:19
  28.1 4.2 copy-start.1
  28.1 4.2 copy-start.2
  28.1 4.2 copy-start.4
  28.1 4.2 copy-start.6
  28.2 4.2 copy-start.7
  28.2 4.2 copy-start.8
  28.2 4.2 copy-start.15
  32.4 260.4 %copy-start = (f32[2,5120,32]{1,2,0:T(8,128)S(1)}, f32[2,5120,32]{1,2,0:T(8,128)}, u32[]{:S(2)}) copy-start(f32[2,5120,32]{1,2,0:T(8,128)} %param.47) | copy-start | bytes 3932164
  304.7 0.7 copy-start.9
  304.7 0.8 copy-start.16
Sparse Core Ops, SparseCore 0:
  304.9 184.8 all-reduce.2
where the time goes:
time: 525 us; the launch traced here: 519 us
  waiting for transfers between devices  182 us (35%)
  matrix products  178 us (34%)
  local copies, waits for them, and re-layouts  49.6 us (9%)
  other arithmetic  45.4 us (9%)
  loops' own time  29.9 us (6%)
  blocking collectives  16.8 us (3%)
  between operations  14.6 us (3%)
    psum x1, waiting for transfers between devices, per_device(): bus_voltage = lax.psum(partial_bus, 'area')  182 us
    dot_general x20, matrix products, advance(): volt = jnp.dot(ginv, right, precision=HIGHEST)  134 us
    dynamic_slice x40, local copies, waits for them, and re-layouts, window(): carry, outward = lax.scan(advance, carry, (incoming, angles))  30 us
    another operation x1, loops' own time, window(): carry, outward = lax.scan(advance, carry, (incoming, angles))  29.9 us
    dynamic_update_slice x20, other arithmetic, window(): carry, outward = lax.scan(advance, carry, (incoming, angles))  13.7 us
    dot_general x20, matrix products, advance(): probe = jnp.dot(picker, volt, precision=HIGHEST)  13.4 us
    broadcast_in_dim x20, other arithmetic, advance(): jnp.where(live, inverter_axial_part * angle_cos_factor - inverter_normal_...  13.1 us
    dot_general x20, matrix products, advance(): right = hist_now + jnp.dot(onehot, stacked, precision=HIGHEST)  12.9 us
  transfers between devices with their start and end apart: 5, of which 2 were waited for; matrix products, arithmetic and copies ran while one was open for 3% of the time, Pallas kernels for 0%

commit v1 on v0

v1 whole, which is shorter than its diff:
```python
import functools
import math

import jax
import jax.numpy as jnp
from jax import lax
from jax.experimental import pallas as pl
from jax.experimental.pallas import tpu as pltpu
from jax.sharding import PartitionSpec as P

STEPS = 20
HIST = 40
SAG_FACTOR = 0.3
F32 = jnp.float32
BF16 = jnp.bfloat16


def shifted(x, by):
    axes = ("area", "row")
    size = lax.axis_size(axes)
    return lax.ppermute(x, axes, [(i, (i + by) % size) for i in range(size)])


def split(x):
    high = x.astype(BF16)
    return high, (x - high.astype(F32)).astype(BF16)


def mm(a, b):
    return lax.dot_general(a, b, (((1,), (0,)), ((), ())), preferred_element_type=F32)


def columns(row, count):
    return jnp.broadcast_to(row, (128, count)).T


def window_kernel(
    lines,
    convs,
    ports,
    reach_ref,
    delay_ref,
    trig_ref,
    count_ref,
    index_ref,
    coef_ref,
    ginv_ref,
    gcap_ref,
    hist_ref,
    below1_ref,
    below2_ref,
    above1_ref,
    above2_ref,
    state_ref,
    target_ref,
    pvolt_ref,
    waves_ref,
    hist_out_ref,
    state_out_ref,
    current_ref,
    big,
    wj,
    wx,
    cap2,
    xs,
):
    nodes = ginv_ref.shape[0]
    probes = 128
    half = lines // 2
    rows = 256

    index = columns(index_ref[...].astype(F32), probes).astype(jnp.int32)
    for c in range(nodes // 128):
        lane = lax.broadcasted_iota(jnp.int32, (probes, 128), 1) + 128 * c
        cap2[:, c * 128 : (c + 1) * 128] = jnp.where(index == lane, 1.0, 0.0)
    pick = cap2[...].astype(BF16)
    scatter = cap2[...].T.astype(BF16)
    for r in range(nodes // rows):
        span = pl.ds(r * rows, rows)
        high, low = split(ginv_ref[span, :])
        big[span, 0:nodes] = high
        big[span, nodes : 2 * nodes] = low
    tail = pl.ds(nodes, probes)
    big[tail, :nodes] = mm(pick, big[0:nodes, 0:nodes]).astype(BF16)
    big[tail, nodes : 2 * nodes] = mm(pick, big[0:nodes, nodes : 2 * nodes]).astype(BF16)
    big[:, 2 * nodes : 2 * nodes + 128] = mm(big[:, 0:nodes], scatter).astype(BF16)
    big[:, 2 * nodes + 128 :] = mm(big[:, nodes : 2 * nodes], scatter).astype(BF16)
    gcap = 2.0 * columns(gcap_ref[...], nodes)

    def put_state(value):
        high, low = split(value)
        wj[:, 0:128] = high
        wj[:, 128:256] = low

    hist_out_ref[...] = hist_ref[...]
    put_state(hist_ref[...])
    state_out_ref[...] = state_ref[...]
    current_ref[...] = jnp.zeros_like(current_ref)
    coef = coef_ref[...]
    two_adm = columns(coef[0:1], 128)[0:lines]
    rate = columns(coef[1:2], 128)[lines : lines + convs]
    limit = columns(coef[2:3], 128)[lines : lines + convs]
    padm = columns(coef[0:1], 128)[lines + convs : lines + convs + ports]
    live = lax.broadcasted_iota(jnp.int32, (convs, 128), 0) < count_ref[0]
    xs[lines + convs + ports :, :] = jnp.zeros((probes - lines - convs - ports, 128), F32)

    def step(t, carry):
        cosine = trig_ref[0, t]
        sine = trig_ref[1, t]
        for l in range(half):
            up = t - delay_ref[l] + HIST
            down = t - delay_ref[l + half] + HIST
            near = reach_ref[l] == 1
            xs[l : l + 1, :] = jnp.where(near, above1_ref[up, l : l + 1, :], above2_ref[up, l : l + 1, :])
            xs[l + half : l + half + 1, :] = jnp.where(
                near, below1_ref[down, l : l + 1, :], below2_ref[down, l : l + 1, :]
            )
        inward = xs[0:lines, :]
        axial = state_out_ref[0]
        normal = state_out_ref[1]
        source = padm * (pvolt_ref[0] * cosine - pvolt_ref[1] * sine)
        xs[lines : lines + convs, :] = jnp.where(live, axial * cosine - normal * sine, 0.0)
        xs[lines + convs : lines + convs + ports, :] = source
        high, low = split(xs[...])
        wx[0:128, 0:128] = high
        wx[128:256, 0:128] = high
        wx[0:128, 128:256] = low
        wx[128:256, 128:256] = low

        def apply(start, size):
            span = pl.ds(start, size)
            both = (
                mm(big[span, 0:nodes], wj[...])
                + mm(big[span, nodes : 2 * nodes], wj[...])
                + mm(big[span, 2 * nodes :], wx[...])
            )
            return both[:, 0:128] + both[:, 128:256]

        probe = apply(nodes, probes)
        volts = apply(0, nodes)
        waves_ref[t] = two_adm * probe[0:lines] - inward
        emf = probe[lines : lines + convs]
        flow = source - padm * probe[lines + convs : lines + convs + ports]
        current_ref[0] += flow * cosine
        current_ref[1] -= flow * sine
        new_axial = axial + rate * (target_ref[0] - axial) - SAG_FACTOR * emf * cosine
        new_normal = normal + rate * (target_ref[1] - normal) + SAG_FACTOR * emf * sine
        state_out_ref[0] = jnp.where(live, limit * jnp.tanh(new_axial / limit), axial)
        state_out_ref[1] = jnp.where(live, limit * jnp.tanh(new_normal / limit), normal)
        after = gcap * volts - hist_out_ref[...]
        hist_out_ref[...] = after
        put_state(after)
        return carry

    lax.fori_loop(0, STEPS, step, 0)
    current_ref[...] = current_ref[...] * (2.0 / STEPS)


def bus_kernel(zt_ref, currents_ref, out_ref, rh, rl):
    @pl.when(pl.program_id(0) == 0)
    def _():
        high, low = split(currents_ref[...])
        rh[...] = high
        rl[...] = low

    zt = zt_ref[...].T
    high, low = split(zt)
    total = mm(high, rh[...]) + mm(low, rh[...]) + mm(high, rl[...])
    out_ref[0] = total[:, 0:128]
    out_ref[1] = total[:, 128:256]


def vmem():
    return pl.BlockSpec(memory_space=pltpu.VMEM)


def smem():
    return pl.BlockSpec(memory_space=pltpu.SMEM)


def per_device(
    conductance_inverse,
    cap_history,
    cap_conductance,
    wave_history,
    line_partner,
    line_node,
    line_delay,
    line_admittance,
    conv_node,
    conv_count,
    conv_state,
    conv_reference,
    conv_rate,
    conv_limit,
    port_node,
    port_admittance,
    port_voltage_prev,
    port_bus,
    transfer_impedance,
):
    subnets = lax.axis_size(("area", "row"))
    own = lax.axis_index(("area", "row"))
    history = wave_history[0]
    lines = history.shape[1]
    half = lines // 2
    cases = history.shape[2]
    nodes = conductance_inverse.shape[1]
    convs = conv_node.shape[1]
    ports = port_node.shape[1]
    upper = history[:, :half]
    lower = history[:, half:]
    below1 = shifted(upper, 1)
    above1 = shifted(lower, -1)
    below2 = shifted(upper, 2)
    above2 = shifted(lower, -2)
    reach = (line_partner[0] - own) % subnets
    zt = jnp.transpose(transfer_impedance, (0, 2, 1))
    zt_all = lax.all_gather(zt, "area", axis=0, tiled=False)

    pad = 128 - lines - convs - ports
    index = jnp.concatenate([line_node, conv_node, port_node, jnp.full((1, pad), -1, jnp.int32)], axis=1)
    ones = jnp.ones((1, 128 - lines - convs), F32)
    coef = jnp.concatenate(
        [
            jnp.concatenate([2.0 * line_admittance, jnp.ones((1, convs), F32), port_admittance, ones[:, :pad]], axis=1),
            jnp.concatenate([jnp.ones((1, lines), F32), conv_rate, ones], axis=1),
            jnp.concatenate([jnp.ones((1, lines), F32), conv_limit, ones], axis=1),
        ],
        axis=0,
    )
    angles = jnp.arange(1, STEPS + 1, dtype=F32) * jnp.float32(2.0 * math.pi / STEPS)
    trig = jnp.stack([jnp.cos(angles), jnp.sin(angles)])
    flops = 2 * STEPS * (nodes + 128) * (2 * nodes + 256) * 256
    waves, hist_end, conv_out, current = pl.pallas_call(
        functools.partial(window_kernel, lines, convs, ports),
        out_shape=(
            jax.ShapeDtypeStruct((STEPS, lines, cases), F32),
            jax.ShapeDtypeStruct((nodes, cases), F32),
            jax.ShapeDtypeStruct((2, convs, cases), F32),
            jax.ShapeDtypeStruct((2, ports, cases), F32),
        ),
        in_specs=[smem()] * 4 + [vmem()] * 12,
        out_specs=(vmem(),) * 4,
        scratch_shapes=[
            pltpu.VMEM((nodes + 128, 2 * nodes + 256), BF16),
            pltpu.VMEM((nodes, 256), BF16),
            pltpu.VMEM((256, 256), BF16),
            pltpu.VMEM((128, nodes), F32),
            pltpu.VMEM((128, 128), F32),
        ],
        cost_estimate=pl.CostEstimate(flops=flops, bytes_accessed=8_000_000, transcendentals=0),
        name="window",
    )(
        reach,
        line_delay[0],
        trig,
        conv_count,
        index,
        coef,
        conductance_inverse[0],
        cap_conductance,
        cap_history[0],
        below1,
        below2,
        above1,
        above2,
        conv_state[0],
        conv_reference[0],
        port_voltage_prev[:, 0],
    )

    areas = lax.axis_size("area")
    rows = lax.axis_size("row")
    bus_rows = transfer_impedance.shape[1]
    members = transfer_impedance.shape[2]
    piece = lax.all_gather(current, ("area", "row"), axis=0, tiled=False)
    piece = piece.reshape(areas, rows, 2, ports, cases).transpose(2, 0, 1, 3, 4).reshape(2, areas, members, cases)
    into_re = jnp.concatenate([piece[0], piece[1]], axis=-1)
    into_im = jnp.concatenate([-piece[1], piece[0]], axis=-1)
    flat = jnp.stack([into_re, into_im], axis=1).reshape(areas * 2 * members, 2 * cases)
    depth = flat.shape[0]
    block = 512
    bus_voltage = pl.pallas_call(
        bus_kernel,
        grid=(bus_rows // block,),
        out_shape=jax.ShapeDtypeStruct((2, bus_rows, cases), F32),
        in_specs=[
            pl.BlockSpec((depth, block), lambda i: (0, i)),
            pl.BlockSpec((depth, 2 * cases), lambda i: (0, 0)),
        ],
        out_specs=pl.BlockSpec((2, block, cases), lambda i: (0, i, 0)),
        scratch_shapes=[pltpu.VMEM((depth, 2 * cases), BF16)] * 2,
        name="buses",
    )(zt_all.reshape(depth, bus_rows), flat)

    local = port_bus.reshape(-1) - lax.axis_index("row") * bus_rows
    inside = (local >= 0) & (local < bus_rows)
    taken = jnp.take(bus_voltage, jnp.clip(local, 0, bus_rows - 1), axis=1)
    taken = jnp.where(inside[None, :, None], taken, 0.0)
    taken = taken.reshape(2, port_bus.shape[0], port_bus.shape[1], cases)
    port_voltage = lax.psum_scatter(taken, "row", scatter_dimension=1, tiled=True)
    return (waves[None], hist_end[None], conv_out[None], bus_voltage, port_voltage)


def solution(mesh):
    both = ("area", "row")
    placed = (
        P(both, None, None),
        P(both, None, None),
        P(both, None),
        P(both, None, None, None),
        P(both, None),
        P(both, None),
        P(both, None),
        P(both, None),
        P(both, None),
        P(both),
        P(both, None, None, None),
        P(both, None, None, None),
        P(both, None),
        P(both, None),
        P(both, None),
        P(both, None),
        P(None, both, None, None),
        P("area", None),
        P(None, "row", "area"),
    )
    return jax.shard_map(
        per_device,
        mesh=mesh,
        in_specs=placed,
        out_specs=(
            P(both, None, None, None),
            P(both, None, None),
            P(both, None, None, None),
            P(None, "row", None),
            P(None, both, None, None),
        ),
        check_vma=False,
    )
```

time: 525 us -> 213 us (0.41)
  matrix products: 178 us -> 0 us
  waiting for transfers between devices: 182 us -> 53.3 us
  Pallas kernels: 0 us -> 50.1 us
  blocking collectives: 16.8 us -> 61.6 us
  other arithmetic: 45.4 us -> 6.97 us
  local copies, waits for them, and re-layouts: 49.6 us -> 17.9 us
  loops' own time: 29.9 us -> 0 us
    psum x1 -> x0, waiting for transfers between devices: 182 us -> none  [per_device(): bus_voltage = lax.psum(partial_bus, 'area')]
    dot_general x66 -> x0, matrix products: 178 us -> none  [the longest x20 134 us: advance(): volt = jnp.dot(ginv, right, precision=HIGHEST)]
    pallas_call x0 -> x2, Pallas kernels: none -> 50.1 us  [the longest x1 37.4 us: per_device(): pl.pallas_call(functools.partial(window_kernel, lines, convs, ports), out...]
    all_gather x1, blocking collectives: 6.37 us -> 51.3 us  [per_device(): piece = lax.all_gather(current, ('area', 'row'), axis=0, tiled=False)]
    all_gather x0 -> x1, waiting for transfers between devices: none -> 42.1 us  [per_device(): zt_all = lax.all_gather(zt, 'area', axis=0, tiled=False)]
    dynamic_slice x40 -> x0, local copies, waits for them, and re-layouts: 30 us -> none  [window(): carry, outward = lax.scan(advance, carry, (incoming, angles))]
    another operation x1 -> x0, loops' own time: 29.9 us -> none  [window(): carry, outward = lax.scan(advance, carry, (incoming, angles))]
    broadcast_in_dim x22 -> x0, other arithmetic: 13.7 us -> none  [the longest x20 13.1 us: advance(): jnp.where(live, inverter_axial_part * angle_cos_factor - inverter_normal_...]
  transfers between devices with their start and end apart: 5 -> 5, of which waited for: 2 -> 5; matrix products, arithmetic and copies ran while one was open for 3% -> 4% of each run, Pallas kernels for 0% -> 18%
where the time goes in v1:
time: 213 us; the launch traced here: 210 us
  blocking collectives  61.6 us (29%)
  waiting for transfers between devices  53.3 us (25%)
  Pallas kernels  50.1 us (24%)
  local copies, waits for them, and re-layouts  17.9 us (8%)
  between operations  14.7 us (7%)
  other arithmetic  6.97 us (3%)
  starting transfers between devices  5.37 us (3%)
    all_gather x1, blocking collectives, per_device(): piece = lax.all_gather(current, ('area', 'row'), axis=0, tiled=False)  51.3 us
    all_gather x1, waiting for transfers between devices, per_device(): zt_all = lax.all_gather(zt, 'area', axis=0, tiled=False)  42.1 us
    pallas_call x1, Pallas kernels, per_device(): pl.pallas_call(functools.partial(window_kernel, lines, convs, ports), out...  37.4 us
    pallas_call x1, Pallas kernels, per_device(): pl.pallas_call(bus_kernel, grid=(bus_rows // block,), out_shape=jax.Shape...  12.7 us
    ppermute x4, waiting for transfers between devices, shifted(): return lax.ppermute(x, axes, [(i, (i + by) % size) for i in range(size)])  10.5 us
    pallas_call x1, local copies, waits for them, and re-layouts, per_device(): pl.pallas_call(bus_kernel, grid=(bus_rows // block,), out_shape=jax.Shape...  10.4 us
    unnamed x1, blocking collectives  10.3 us
    ppermute x4, starting transfers between devices, shifted(): return lax.ppermute(x, axes, [(i, (i + by) % size) for i in range(size)])  5.33 us
  transfers between devices with their start and end apart: 5, of which 5 were waited for; matrix products, arithmetic and copies ran while one was open for 4% of the time, Pallas kernels for 18%

profile of v1, /device:TPU:20, one launch (start us, length us, event | category | flops | bytes accessed | tf_op | source)
XLA Modules:
  0.0 210.0 jit_solution(6502670194100674158)
XLA Ops:
  7.2 0.0 all-gather.4.cloned.1.call-start
  7.2 0.7 all-gather.4.cloned.1.call-update
  7.9 1.1 fusion.6
  9.0 0.1 collective-permute-start
  9.1 1.5 collective-permute-start.1
  10.6 1.4 collective-permute-start.2
  12.0 2.4 %collective-permute-start.3 = (f32[40,16,128]{2,1,0:T(8,128)S(1)}, f32[40,16,128]{2,1,0:T(8,128)S(1)}, u32[]{:S(2)}, u32[]{:S(2)}) collective-permute-start(f32[40,16,128]{2,1,0:T(8,128)S(1)} %get-tuple-element.15), channel_id=1, source_target_pairs={{0,30},{1,31},{2,0},{3,1},{4,2},{5,3},{6,4},{7,5},{8,6},{9,7},{10,... | collective-permute-start | bytes 983048 | tf_op jit(solution)/shard_map/ppermute | solution.py:21
  15.0 0.7 compare_and_fusion
  15.7 0.1 min.12
  15.8 1.3 dynamic-slice
  17.2 0.6 pad_maximum_fusion.1.trig_ref
  17.8 0.7 broadcast_multiply_fusion
  18.4 1.4 maximum_maximum_fusion.coef_ref
  19.8 1.4 bitcast_add_fusion.index_ref
  21.2 1.2 and_select_fusion.reach_ref
  22.4 4.7 %collective-permute-done.below1_ref = f32[40,16,128]{2,1,0:T(8,128)S(1)} collective-permute-done((f32[40,16,128]{2,1,0:T(8,128)S(1)}, f32[40,16,128]{2,1,0:T(8,128)S(1)}, u32[]{:S(2)}, u32[]{:S(2)}) %collective-permute-start) | collective-permute-done | bytes 327712 | tf_op jit(solution)/shard_map/ppermute | solution.py:21
  27.2 0.0 copy-start
  27.2 1.9 collective-permute-done.1.below2_ref
  29.1 0.0 copy-start.1
  29.1 0.4 collective-permute-done.2.above1_ref
  29.5 0.0 copy-start.2
  29.5 3.5 %collective-permute-done.3.above2_ref = f32[40,16,128]{2,1,0:T(8,128)S(1)} collective-permute-done((f32[40,16,128]{2,1,0:T(8,128)S(1)}, f32[40,16,128]{2,1,0:T(8,128)S(1)}, u32[]{:S(2)}, u32[]{:S(2)}) %collective-permute-start.3) | collective-permute-done | bytes 327712 | tf_op jit(solution)/shard_map/ppermute | solution.py:21
  33.0 0.0 copy-start.3
  33.0 0.0 copy-done
  33.0 0.0 copy-done.1
  33.0 0.0 copy-done.2
  33.0 0.7 copy-done.3
  33.7 37.4 %window.1 = (f32[20,32,128]{2,1,0:T(8,128)}, f32[1024,128]{1,0:T(8,128)}, f32[2,64,128]{2,1,0:T(8,128)}, f32[2,8,128]{2,1,0:T(8,128)}) custom-call(s32[32]{0:T(128)} %and_select_fusion.reach_ref, s32[32]{0:T(128)} %bitcast.52, f32[2,20]{1,0:T(2,128)} %pad_maximum_fusion.1.trig_ref, s32[1]{0:T(128)S(6)} %copy.36.count_ref, ...), custom_call_target="tpu_custom_call" | custom-call | flops 27179089920 | bytes 8000000 | tf_op jit(solution)/shard_map/window/pallas_call | solution.py:235
  71.1 51.3 %all-gather.1 = f32[64,8,128]{2,1,0:T(8,128)S(1)} all-gather(f32[2,8,128]{2,1,0:T(8,128)} %get-tuple-element.12), channel_id=3, replica_groups=mesh['area'=8,'row'=4] {'area','row'}, dimensions={0}, use_global_device_ids=true | all-gather | bytes 270336 | tf_op jit(solution)/shard_map/all_gather | solution.py:277
  122.5 0.8 pad_maximum_fusion
  123.3 42.1 %all-gather.4.cloned.1.call-done = f32[16,32,5120]{2,1,0:T(8,128)} async-done(((f32[2,32,5120]{2,1,0:T(8,128)}), f32[16,32,5120]{2,1,0:T(8,128)}) %all-gather.4.cloned.1.call-update) | async-done | bytes 10485776 | tf_op jit(solution)/shard_map/all_gather | solution.py:219
  165.4 12.7 %buses.1 = f32[2,5120,128]{2,1,0:T(8,128)} custom-call(f32[512,5120]{1,0:T(8,128)} %bitcast.40, f32[512,256]{1,0:T(8,128)} %bitcast.41), custom_call_target="tpu_custom_call" | custom-call | tf_op jit(solution)/shard_map/buses/pallas_call | solution.py:284
  178.1 10.4 %copy.29 = f32[2,5120,128]{2,0,1:T(2,128)} copy(f32[2,5120,128]{2,1,0:T(8,128)} %buses.1) | data formatting | bytes 10485760 | tf_op jit(solution)/shard_map/buses/pallas_call | solution.py:284
  188.5 3.1 %gather_fusion = f32[32,2,128]{2,1,0:T(2,128)S(1)} fusion(f32[2,5120,128]{2,0,1:T(2,128)} %copy.29, s32[1024]{0:T(1024)S(1)} %pad_clamp_fusion), kind=kCustom, calls=%fused_computation | custom fusion | bytes 65664 | tf_op jit(solution)/shard_map/jit(_take)/gather | solution.py:299
  191.6 0.1 fusion
  191.7 10.3 %all-reduce = f32[2,4,8,128]{3,2,1,0:T(8,128)S(1)} all-reduce(f32[2,4,8,128]{3,2,1,0:T(8,128)S(1)} %fusion), channel_id=4, replica_groups=mesh['area'=8,'row'=4] {'row'}, use_global_device_ids=true, to_apply=%region_0.1.clone | all-reduce | flops 8192 | bytes 65536
  201.9 1.2 constant_dynamic-slice_fusion
  (10 shorter events, 0.1 us)
Async XLA Ops:
  7.2 158.2 %all-gather.4.cloned.1.call-start = ((), (), s32[]{:S(2)}) async-start(), calls=%async_computation | async-start | bytes 11796480 | tf_op jit(solution)/shard_map/all_gather | solution.py:219
  9.0 18.1 %collective-permute-start = (f32[40,16,128]{2,1,0:T(8,128)S(1)}, f32[40,16,128]{2,1,0:T(8,128)S(1)}, u32[]{:S(2)}, u32[]{:S(2)}) collective-permute-start(f32[40,16,128]{2,1,0:T(8,128)S(1)} %get-tuple-element.16), channel_id=1, source_target_pairs={{0,1},{1,2},{2,3},{3,4},{4,5},{5,6},{6,7},{7,8},{8,9},{9,10},{10,1... | collective-permute-start | bytes 983048 | tf_op jit(solution)/shard_map/ppermute | solution.py:21
  9.1 20.0 %collective-permute-start.1 = (f32[40,16,128]{2,1,0:T(8,128)S(1)}, f32[40,16,128]{2,1,0:T(8,128)S(1)}, u32[]{:S(2)}, u32[]{:S(2)}) collective-permute-start(f32[40,16,128]{2,1,0:T(8,128)S(1)} %get-tuple-element.16), channel_id=1, source_target_pairs={{0,2},{1,3},{2,4},{3,5},{4,6},{5,7},{6,8},{7,9},{8,10},{9,11},{10,... | collective-permute-start | bytes 983048 | tf_op jit(solution)/shard_map/ppermute | solution.py:21
  10.6 18.9 %collective-permute-start.2 = (f32[40,16,128]{2,1,0:T(8,128)S(1)}, f32[40,16,128]{2,1,0:T(8,128)S(1)}, u32[]{:S(2)}, u32[]{:S(2)}) collective-permute-start(f32[40,16,128]{2,1,0:T(8,128)S(1)} %get-tuple-element.15), channel_id=1, source_target_pairs={{0,31},{1,0},{2,1},{3,2},{4,3},{5,4},{6,5},{7,6},{8,7},{9,8},{10,9... | collective-permute-start | bytes 983048 | tf_op jit(solution)/shard_map/ppermute | solution.py:21
  12.0 21.0 %collective-permute-start.3 = (f32[40,16,128]{2,1,0:T(8,128)S(1)}, f32[40,16,128]{2,1,0:T(8,128)S(1)}, u32[]{:S(2)}, u32[]{:S(2)}) collective-permute-start(f32[40,16,128]{2,1,0:T(8,128)S(1)} %get-tuple-element.15), channel_id=1, source_target_pairs={{0,30},{1,31},{2,0},{3,1},{4,2},{5,3},{6,4},{7,5},{8,6},{9,7},{10,... | collective-permute-start | bytes 983048 | tf_op jit(solution)/shard_map/ppermute | solution.py:21
  27.2 5.8 %copy-start = (f32[40,16,128]{2,1,0:T(8,128)}, f32[40,16,128]{2,1,0:T(8,128)S(1)}, u32[]{:S(2)}) copy-start(f32[40,16,128]{2,1,0:T(8,128)S(1)} %collective-permute-done.below1_ref) | copy-start | bytes 983044
  29.1 3.9 %copy-start.1 = (f32[40,16,128]{2,1,0:T(8,128)}, f32[40,16,128]{2,1,0:T(8,128)S(1)}, u32[]{:S(2)}) copy-start(f32[40,16,128]{2,1,0:T(8,128)S(1)} %collective-permute-done.1.below2_ref) | copy-start | bytes 983044
  29.5 3.5 %copy-start.2 = (f32[40,16,128]{2,1,0:T(8,128)}, f32[40,16,128]{2,1,0:T(8,128)S(1)}, u32[]{:S(2)}) copy-start(f32[40,16,128]{2,1,0:T(8,128)S(1)} %collective-permute-done.2.above1_ref) | copy-start | bytes 983044
  33.0 0.7 copy-start.3
Sparse Core Ops, SparseCore 0:
  10.2 155.2 all-gather.3

commit v2 on v1

--- a/solution.py
+++ b/solution.py
@@ -13,6 +13,7 @@
 SAG_FACTOR = 0.3
 F32 = jnp.float32
 BF16 = jnp.bfloat16
+MESH = pl.DeviceIdType.MESH
 
 
 def shifted(x, by):
@@ -54,20 +55,65 @@
     state_ref,
     target_ref,
     pvolt_ref,
+    zc_ref,
     waves_ref,
     hist_out_ref,
     state_out_ref,
-    current_ref,
+    flat_ref,
+    bus_ref,
     big,
     wj,
     wx,
     cap2,
     xs,
+    current_ref,
+    zin,
+    cin,
+    mine,
+    rh,
+    rl,
+    zs,
+    zr,
+    rs,
+    rr,
+    cs,
+    cr,
+    zlocal,
+    os,
+    orr,
+    fs,
+    fr,
+    olocal,
 ):
     nodes = ginv_ref.shape[0]
     probes = 128
     half = lines // 2
     rows = 256
+    areas, group = cin.shape[0], cin.shape[1]
+    depth, chunk = zin.shape[1], zin.shape[2]
+    a = lax.axis_index("area")
+    r = lax.axis_index("row")
+
+    barrier = pltpu.get_barrier_semaphore()
+    for d in range(1, areas):
+        pl.semaphore_signal(barrier, inc=1, device_id=(lax.rem(a + d, areas), r), device_id_type=MESH)
+    for d in range(1, group):
+        pl.semaphore_signal(barrier, inc=1, device_id=(a, lax.rem(r + d, group)), device_id_type=MESH)
+    pl.semaphore_wait(barrier, areas + group - 2)
+
+    def send(src, dst, ssem, rsem, to):
+        return pltpu.make_async_remote_copy(
+            src_ref=src, dst_ref=dst, send_sem=ssem, recv_sem=rsem, device_id=to, device_id_type=MESH
+        )
+
+    own_z = pltpu.make_async_copy(zc_ref.at[a], zin.at[a], zlocal)
+    own_z.start()
+    z_copies = []
+    for d in range(1, areas):
+        to = lax.rem(a + d, areas)
+        copy = send(zc_ref.at[to], zin.at[a], zs.at[d], zr.at[d], (to, r))
+        copy.start()
+        z_copies.append(copy)
 
     index = columns(index_ref[...].astype(F32), probes).astype(jnp.int32)
     for c in range(nodes // 128):
@@ -75,8 +121,8 @@
         cap2[:, c * 128 : (c + 1) * 128] = jnp.where(index == lane, 1.0, 0.0)
     pick = cap2[...].astype(BF16)
     scatter = cap2[...].T.astype(BF16)
-    for r in range(nodes // rows):
-        span = pl.ds(r * rows, rows)
+    for b in range(nodes // rows):
+        span = pl.ds(b * rows, rows)
         high, low = split(ginv_ref[span, :])
         big[span, 0:nodes] = high
         big[span, nodes : 2 * nodes] = low
@@ -108,8 +154,8 @@
         cosine = trig_ref[0, t]
         sine = trig_ref[1, t]
         for l in range(half):
-            up = t - delay_ref[l] + HIST
-            down = t - delay_ref[l + half] + HIST
+            up = jnp.clip(t - delay_ref[l] + HIST, 0, HIST - 1)
+            down = jnp.clip(t - delay_ref[l + half] + HIST, 0, HIST - 1)
             near = reach_ref[l] == 1
             xs[l : l + 1, :] = jnp.where(near, above1_ref[up, l : l + 1, :], above2_ref[up, l : l + 1, :])
             xs[l + half : l + half + 1, :] = jnp.where(
@@ -153,21 +199,84 @@
         return carry
 
     lax.fori_loop(0, STEPS, step, 0)
-    current_ref[...] = current_ref[...] * (2.0 / STEPS)
-
-
-def bus_kernel(zt_ref, currents_ref, out_ref, rh, rl):
-    @pl.when(pl.program_id(0) == 0)
-    def _():
-        high, low = split(currents_ref[...])
-        rh[...] = high
-        rl[...] = low
-
-    zt = zt_ref[...].T
-    high, low = split(zt)
+    cin[a, r] = current_ref[...] * (2.0 / STEPS)
+
+    copies = []
+    for d in range(1, group):
+        block = cin.at[a, r]
+        copy = send(block, block, rs.at[d], rr.at[d], (a, lax.rem(r + d, group)))
+        copy.start()
+        copies.append(copy)
+    for copy in copies:
+        copy.wait()
+    copies = []
+    for d in range(1, areas):
+        block = cin.at[a]
+        copy = send(block, block, cs.at[d], cr.at[d], (lax.rem(a + d, areas), r))
+        copy.start()
+        copies.append(copy)
+    own_z.wait()
+    for copy in z_copies:
+        copy.wait()
+    for copy in copies:
+        copy.wait()
+    members = group * ports
+    for i in range(areas):
+        for j in range(group):
+            re, im = cin[i, j, 0], cin[i, j, 1]
+            top = i * depth + j * ports
+            flat_ref[top : top + ports, 0:128] = re
+            flat_ref[top : top + ports, 128:256] = im
+            flat_ref[top + members : top + members + ports, 0:128] = -im
+            flat_ref[top + members : top + members + ports, 128:256] = re
+    high, low = split(flat_ref[...])
+    rh[...] = high
+    rl[...] = low
+    high, low = split(zin[...].reshape(areas * depth, chunk).T)
     total = mm(high, rh[...]) + mm(low, rh[...]) + mm(high, rl[...])
-    out_ref[0] = total[:, 0:128]
-    out_ref[1] = total[:, 128:256]
+    mine[0] = total[:, 0:128]
+    mine[1] = total[:, 128:256]
+
+    inner = 2 ** ((areas.bit_length() - 1) // 2)
+    outer = areas // inner
+    zi = lax.div(a, inner)
+    xi = lax.rem(a, inner)
+
+    def region(part, who):
+        return bus_ref.at[part, pl.ds(pl.multiple_of(who * chunk, 8), chunk), :]
+
+    pending = []
+    arrivals = []
+    for part in range(2):
+        local = pltpu.make_async_copy(mine.at[part], region(part, a), olocal.at[part])
+        local.start()
+        pending.append(local)
+        for d in range(1, inner):
+            to = zi * inner + lax.rem(xi + d, inner)
+            k = part * areas + d
+            copy = send(mine.at[part], region(part, a), os.at[k], orr.at[k], (to, r))
+            copy.start()
+            pending.append(copy)
+        for d in range(1, outer):
+            to = lax.rem(zi + d, outer) * inner + xi
+            k = part * areas + inner * d
+            copy = send(mine.at[part], region(part, a), os.at[k], orr.at[k], (to, r))
+            copy.start()
+            arrivals.append((part, d, copy))
+    for part, d, copy in arrivals:
+        copy.wait_recv()
+        source = lax.rem(zi + outer - d, outer) * inner + xi
+        for e in range(1, inner):
+            to = zi * inner + lax.rem(xi + e, inner)
+            k = part * areas + inner * d + e
+            block = region(part, source)
+            forward = send(block, block, fs.at[k], fr.at[k], (to, r))
+            forward.start()
+            pending.append(forward)
+    for _, _, copy in arrivals:
+        copy.wait_send()
+    for copy in pending:
+        copy.wait()
 
 
 def vmem():
@@ -215,8 +324,20 @@
     below2 = shifted(upper, 2)
     above2 = shifted(lower, -2)
     reach = (line_partner[0] - own) % subnets
-    zt = jnp.transpose(transfer_impedance, (0, 2, 1))
-    zt_all = lax.all_gather(zt, "area", axis=0, tiled=False)
+    areas = lax.axis_size("area")
+    group = lax.axis_size("row")
+    bus_rows = transfer_impedance.shape[1]
+    members = transfer_impedance.shape[2]
+    chunk = bus_rows // areas
+    zt = jnp.transpose(transfer_impedance, (0, 2, 1)).reshape(2 * members, bus_rows)
+    zc = jnp.transpose(zt.reshape(2 * members, areas, chunk), (1, 0, 2))
+    all_bus = lax.all_gather(port_bus, "area", axis=0, tiled=False).reshape(-1)
+    local = all_bus - lax.axis_index("row") * bus_rows
+    pick = (jnp.arange(bus_rows, dtype=jnp.int32)[:, None] == local[None, :]).astype(F32)
+    picked = jnp.dot(zt, pick, precision=lax.Precision.HIGHEST).reshape(2 * members, areas, group, ports)
+    picked = lax.psum_scatter(picked, "row", scatter_dimension=2, tiled=True).reshape(2 * members, areas * ports)
+    picked = lax.all_gather(picked, "area", axis=0, tiled=True)
+    zport = lax.dynamic_slice_in_dim(picked, lax.axis_index("area") * ports, ports, 1)
 
     pad = 128 - lines - convs - ports
     index = jnp.concatenate([line_node, conv_node, port_node, jnp.full((1, pad), -1, jnp.int32)], axis=1)
@@ -232,23 +353,43 @@
     angles = jnp.arange(1, STEPS + 1, dtype=F32) * jnp.float32(2.0 * math.pi / STEPS)
     trig = jnp.stack([jnp.cos(angles), jnp.sin(angles)])
     flops = 2 * STEPS * (nodes + 128) * (2 * nodes + 256) * 256
-    waves, hist_end, conv_out, current = pl.pallas_call(
+    waves, hist_end, conv_out, flat, bus_voltage = pl.pallas_call(
         functools.partial(window_kernel, lines, convs, ports),
         out_shape=(
             jax.ShapeDtypeStruct((STEPS, lines, cases), F32),
             jax.ShapeDtypeStruct((nodes, cases), F32),
             jax.ShapeDtypeStruct((2, convs, cases), F32),
-            jax.ShapeDtypeStruct((2, ports, cases), F32),
+            jax.ShapeDtypeStruct((areas * 2 * members, 2 * cases), F32),
+            jax.ShapeDtypeStruct((2, bus_rows, cases), F32),
         ),
-        in_specs=[smem()] * 4 + [vmem()] * 12,
-        out_specs=(vmem(),) * 4,
+        in_specs=[smem()] * 4 + [vmem()] * 12 + [pl.BlockSpec(memory_space=pl.ANY)],
+        out_specs=(vmem(),) * 4 + (pl.BlockSpec(memory_space=pl.ANY),),
         scratch_shapes=[
             pltpu.VMEM((nodes + 128, 2 * nodes + 256), BF16),
             pltpu.VMEM((nodes, 256), BF16),
             pltpu.VMEM((256, 256), BF16),
             pltpu.VMEM((128, nodes), F32),
             pltpu.VMEM((128, 128), F32),
+            pltpu.VMEM((2, ports, cases), F32),
+            pltpu.VMEM((areas, 2 * members, chunk), F32),
+            pltpu.VMEM((areas, group, 2, ports, cases), F32),
+            pltpu.VMEM((2, chunk, cases), F32),
+            pltpu.VMEM((areas * 2 * members, 2 * cases), BF16),
+            pltpu.VMEM((areas * 2 * members, 2 * cases), BF16),
+            pltpu.SemaphoreType.DMA((areas,)),
+            pltpu.SemaphoreType.DMA((areas,)),
+            pltpu.SemaphoreType.DMA((group,)),
+            pltpu.SemaphoreType.DMA((group,)),
+            pltpu.SemaphoreType.DMA((areas,)),
+            pltpu.SemaphoreType.DMA((areas,)),
+            pltpu.SemaphoreType.DMA,
+            pltpu.SemaphoreType.DMA((2 * areas,)),
+            pltpu.SemaphoreType.DMA((2 * areas,)),
+            pltpu.SemaphoreType.DMA((2 * areas,)),
+            pltpu.SemaphoreType.DMA((2 * areas,)),
+            pltpu.SemaphoreType.DMA((2,)),
         ],
+        compiler_params=pltpu.CompilerParams(collective_id=0, has_side_effects=True),
         cost_estimate=pl.CostEstimate(flops=flops, bytes_accessed=8_000_000, transcendentals=0),
         name="window",
     )(
@@ -268,38 +409,11 @@
         conv_state[0],
         conv_reference[0],
         port_voltage_prev[:, 0],
+        zc,
     )
 
-    areas = lax.axis_size("area")
-    rows = lax.axis_size("row")
-    bus_rows = transfer_impedance.shape[1]
-    members = transfer_impedance.shape[2]
-    piece = lax.all_gather(current, ("area", "row"), axis=0, tiled=False)
-    piece = piece.reshape(areas, rows, 2, ports, cases).transpose(2, 0, 1, 3, 4).reshape(2, areas, members, cases)
-    into_re = jnp.concatenate([piece[0], piece[1]], axis=-1)
-    into_im = jnp.concatenate([-piece[1], piece[0]], axis=-1)
-    flat = jnp.stack([into_re, into_im], axis=1).reshape(areas * 2 * members, 2 * cases)
-    depth = flat.shape[0]
-    block = 512
-    bus_voltage = pl.pallas_call(
-        bus_kernel,
-        grid=(bus_rows // block,),
-        out_shape=jax.ShapeDtypeStruct((2, bus_rows, cases), F32),
-        in_specs=[
-            pl.BlockSpec((depth, block), lambda i: (0, i)),
-            pl.BlockSpec((depth, 2 * cases), lambda i: (0, 0)),
-        ],
-        out_specs=pl.BlockSpec((2, block, cases), lambda i: (0, i, 0)),
-        scratch_shapes=[pltpu.VMEM((depth, 2 * cases), BF16)] * 2,
-        name="buses",
-    )(zt_all.reshape(depth, bus_rows), flat)
-
-    local = port_bus.reshape(-1) - lax.axis_index("row") * bus_rows
-    inside = (local >= 0) & (local < bus_rows)
-    taken = jnp.take(bus_voltage, jnp.clip(local, 0, bus_rows - 1), axis=1)
-    taken = jnp.where(inside[None, :, None], taken, 0.0)
-    taken = taken.reshape(2, port_bus.shape[0], port_bus.shape[1], cases)
-    port_voltage = lax.psum_scatter(taken, "row", scatter_dimension=1, tiled=True)
+    seen = lax.dot_general(zport, flat, (((0,), (0,)), ((), ())), precision=lax.Precision.HIGHEST)
+    port_voltage = jnp.stack([seen[:, :cases], seen[:, cases:]])[:, None]
     return (waves[None], hist_end[None], conv_out[None], bus_voltage, port_voltage)
 
 

time: 213 us -> 257 us (1.21); the launches traced: 210 us -> 257 us
  Pallas kernels: 50.1 us -> 133 us
  waiting for transfers between devices: 53.3 us -> 25.3 us
  other arithmetic: 6.97 us -> 3.1 us
  matrix products: 0 us -> 3.8 us
  blocking collectives: 61.6 us -> 58.5 us
  local copies, waits for them, and re-layouts: 17.9 us -> 15.1 us
    pallas_call x1, Pallas kernels: 37.4 us -> 133 us  [per_device(): pl.pallas_call(functools.partial(window_kernel, lines, convs, ports), out...]
    all_gather x1 -> x0, waiting for transfers between devices: 42.1 us -> none  [per_device(): zt_all = lax.all_gather(zt, 'area', axis=0, tiled=False)]
    unnamed x1 -> x2, waiting for transfers between devices: 0.68 us -> 25.3 us
    pallas_call x1 -> x0, Pallas kernels: 12.7 us -> none  [per_device(): pl.pallas_call(bus_kernel, grid=(bus_rows // block,), out_shape=jax.Shape...]
    ppermute x4, waiting for transfers between devices: 10.5 us -> 0.01 us  [shifted(): return lax.ppermute(x, axes, [(i, (i + by) % size) for i in range(size)])]
    pallas_call x1 -> x0, local copies, waits for them, and re-layouts: 10.4 us -> none  [per_device(): pl.pallas_call(bus_kernel, grid=(bus_rows // block,), out_shape=jax.Shape...]
    unnamed x1 -> x0, blocking collectives: 10.3 us -> none
    all_gather x1 -> x2, blocking collectives: 51.3 us -> 58.5 us  [the longest x1 32.2 us: per_device(): all_bus = lax.all_gather(port_bus, 'area', axis=0, tiled=False).reshape(-1)]
  transfers between devices with their start and end apart: 5 -> 5, of which waited for: 5 -> 1; matrix products, arithmetic and copies ran while one was open for 4% -> 3% of each run, Pallas kernels for 18% -> 0%
where the time goes in v2:
time: 257 us
  Pallas kernels  133 us (52%)
  blocking collectives  58.5 us (23%)
  waiting for transfers between devices  25.3 us (10%)
  local copies, waits for them, and re-layouts  15.1 us (6%)
  between operations  14.9 us (6%)
  matrix products  3.8 us (1%)
  starting transfers between devices  3.24 us (1%)
  other arithmetic  3.1 us (1%)
    pallas_call x1, Pallas kernels, per_device(): pl.pallas_call(functools.partial(window_kernel, lines, convs, ports), out...  133 us
    all_gather x1, blocking collectives, per_device(): all_bus = lax.all_gather(port_bus, 'area', axis=0, tiled=False).reshape(-1)  32.2 us
    all_gather x1, blocking collectives, per_device(): picked = lax.all_gather(picked, 'area', axis=0, tiled=True)  26.3 us
    unnamed x2, waiting for transfers between devices  25.3 us
    unnamed x40, local copies, waits for them, and re-layouts  10.2 us
  transfers between devices with their start and end apart: 5, of which 1 were waited for; matrix products, arithmetic and copies ran while one was open for 3% of the time, Pallas kernels for 0%

profile of v2, /device:TPU:20, one launch (start us, length us, event | category | flops | bytes accessed | tf_op | source)
XLA Modules:
  0.0 256.8 jit_solution(8490534561902085344)
XLA Ops:
  7.2 0.0 copy-start.3
  7.2 0.0 copy-start
  7.2 0.0 all-reduce.3.cloned.1.call-start
  7.2 1.2 fusion.9
  8.5 0.0 copy-start.14
  8.5 0.0 copy-start.15
  8.5 0.0 copy-start.7
  8.5 0.0 copy-start.8
  8.5 0.0 copy-start.9
  8.5 0.0 copy-start.4
  8.5 0.0 copy-start.5
  8.5 0.0 copy-start.6
  8.6 0.6 collective-permute-start.3
  9.1 1.5 collective-permute-start.2
  10.6 0.9 collective-permute-start.1
  11.5 0.2 collective-permute-start
  11.8 0.0 copy-done.3
  11.8 32.2 %all-gather.1 = s32[8,4,8]{2,1,0:T(4,128)S(1)} all-gather(s32[1,4,8]{2,1,0:T(4,128)S(1)} %bitcast.57), channel_id=2, replica_groups=mesh['area'=8,'row'=4] {'area'}, dimensions={0}, use_global_device_ids=true | all-gather | bytes 1152 | tf_op jit(solution)/shard_map/all_gather | solution.py:334
  44.0 0.1 sub.27
  44.1 0.0 copy-done
  44.1 2.1 fusion.2
  46.1 0.8 copy.29
  46.9 0.0 all-reduce.3.cloned.1.call-update
  47.0 0.0 copy-done.14
  47.0 0.0 copy-done.15
  47.0 0.5 and_select_fusion.reach_ref
  47.6 0.0 copy-done.7
  47.6 0.0 copy-done.8
  47.6 0.0 copy-done.9
  47.6 0.7 maximum_maximum_fusion.coef_ref
  48.2 0.6 pad_maximum_fusion.trig_ref
  48.8 0.0 copy-done.4
  48.8 0.0 copy-done.5
  48.8 0.0 copy-done.6
  48.8 0.7 bitcast_add_fusion.index_ref
  50.1 0.2 copy.34
  50.4 0.0 copy-start.16
  50.4 1.3 copy.36
  51.7 0.0 copy-done.16
  51.7 0.6 dynamic-slice
  52.3 25.3 %all-reduce.3.cloned.1.call-done = f32[64,8,4,8]{0,3,2,1:T(8,128)} async-done(((f32[64,8,4,8]{0,3,2,1:T(8,128)}), f32[64,8,4,8]{0,3,2,1:T(8,128)}) %all-reduce.3.cloned.1.call-update) | async-done | bytes 65552
  77.5 1.4 dynamic-slice_bitcast_fusion
  78.9 0.1 copy.30
  79.0 26.3 %all_gather.11 = f32[512,64]{1,0:T(8,128)S(1)} all-gather(f32[64,64]{1,0:T(8,128)S(1)} %copy.30), channel_id=1, replica_groups=mesh['area'=8,'row'=4] {'area'}, dimensions={0}, use_global_device_ids=true | all-gather | bytes 147456 | tf_op jit(solution)/shard_map/all_gather | solution.py:339
  105.3 0.0 collective-permute-done.3.above2_ref
  105.3 0.0 collective-permute-done.2.above1_ref
  105.3 0.0 copy-start.11
  105.3 0.0 collective-permute-done.1.below2_ref
  105.3 0.0 copy-start.12
  105.3 0.0 collective-permute-done.below1_ref
  105.3 0.0 copy-start.13
  105.4 0.7 copy-done.10
  106.0 0.1 copy-done.11
  106.1 0.1 copy-done.12
  106.2 0.1 copy-done.13
  106.3 132.9 %window.1 = (f32[20,32,128]{2,1,0:T(8,128)}, f32[1024,128]{1,0:T(8,128)}, f32[2,64,128]{2,1,0:T(8,128)}, f32[512,256]{1,0:T(8,128)}, f32[2,5120,128]{2,1,0:T(8,128)}) custom-call(s32[32]{0:T(128)} %and_select_fusion.reach_ref, s32[32]{0:T(128)} %bitcast.63, f32[2,20]{1,0:T(2,128)} %pad_maximum_fusion.trig_ref, s32[1]{0:T(128)S(6)} %copy.42.count_ref, ...), custom_call_target="tpu_custom_call" | custom-call | flops 27179089920 | bytes 8000000 | tf_op jit(solution)/shard_map/window/pallas_call | solution.py:356
  239.3 0.0 copy-start.1
  239.3 0.0 copy-start.2
  239.3 1.8 fusion.3
  241.0 0.6 maximum_bitcast_fusion
  241.7 1.7 copy.43
  243.4 0.8 copy.44
  244.2 0.6 copy.45
  244.8 5.2 %copy.46 = f32[2,5120,128]{2,1,0:T(8,128)} copy(f32[2,5120,128]{2,1,0:T(8,128)} %get-tuple-element.44) | data formatting | bytes 10485760
  (11 shorter events, 0.1 us)
Async XLA Ops:
  7.2 4.6 %copy-start.3 = (s32[4,8]{1,0:T(4,128)S(1)}, s32[4,8]{1,0:T(4,128)}, u32[]{:S(2)}) copy-start(s32[4,8]{1,0:T(4,128)} %param.36) | copy-start | bytes 388
  7.2 36.9 %copy-start = (f32[2,5120,32]{1,2,0:T(8,128)S(1)}, f32[2,5120,32]{1,2,0:T(8,128)}, u32[]{:S(2)}) copy-start(f32[2,5120,32]{1,2,0:T(8,128)} %param.37) | copy-start | bytes 3932164
  7.2 70.4 %all-reduce.3.cloned.1.call-start = ((), (), s32[]{:S(2)}) async-start(), calls=%async_computation | async-start | bytes 262144
  8.5 38.5 %copy-start.14 = (f32[1,32]{1,0:T(1,128)S(1)}, f32[1,32]{1,0:T(1,128)}, u32[]{:S(2)}) copy-start(f32[1,32]{1,0:T(1,128)} %param.26) | copy-start | bytes 388
  8.5 38.5 %copy-start.15 = (s32[1,32]{1,0:T(1,128)S(1)}, s32[1,32]{1,0:T(1,128)}, u32[]{:S(2)}) copy-start(s32[1,32]{1,0:T(1,128)} %param.23) | copy-start | bytes 388
  8.5 39.1 %copy-start.7 = (f32[1,64]{1,0:T(1,128)S(1)}, f32[1,64]{1,0:T(1,128)}, u32[]{:S(2)}) copy-start(f32[1,64]{1,0:T(1,128)} %param.32) | copy-start | bytes 772
  8.5 39.1 %copy-start.8 = (f32[1,64]{1,0:T(1,128)S(1)}, f32[1,64]{1,0:T(1,128)}, u32[]{:S(2)}) copy-start(f32[1,64]{1,0:T(1,128)} %param.31) | copy-start | bytes 772
  8.5 39.1 %copy-start.9 = (f32[1,8]{1,0:T(1,128)S(1)}, f32[1,8]{1,0:T(1,128)}, u32[]{:S(2)}) copy-start(f32[1,8]{1,0:T(1,128)} %param.34) | copy-start | bytes 100
  8.5 40.3 %copy-start.4 = (s32[1,8]{1,0:T(1,128)S(1)}, s32[1,8]{1,0:T(1,128)}, u32[]{:S(2)}) copy-start(s32[1,8]{1,0:T(1,128)} %param.33) | copy-start | bytes 100
  8.5 40.3 %copy-start.5 = (s32[1,64]{1,0:T(1,128)S(1)}, s32[1,64]{1,0:T(1,128)}, u32[]{:S(2)}) copy-start(s32[1,64]{1,0:T(1,128)} %param.27) | copy-start | bytes 772
  8.5 40.3 %copy-start.6 = (s32[1,32]{1,0:T(1,128)S(1)}, s32[1,32]{1,0:T(1,128)}, u32[]{:S(2)}) copy-start(s32[1,32]{1,0:T(1,128)} %param.24) | copy-start | bytes 388
  8.6 96.7 %collective-permute-start.3 = (f32[40,16,128]{2,1,0:T(8,128)S(1)}, f32[40,16,128]{2,1,0:T(8,128)S(1)}, u32[]{:S(2)}, u32[]{:S(2)}) collective-permute-start(f32[40,16,128]{2,1,0:T(8,128)S(1)} %get-tuple-element.30), channel_id=1, source_target_pairs={{0,30},{1,31},{2,0},{3,1},{4,2},{5,3},{6,4},{7,5},{8,6},{9,7},{10,... | collective-permute-start | bytes 983048 | tf_op jit(solution)/shard_map/ppermute | solution.py:22
  9.1 96.2 %collective-permute-start.2 = (f32[40,16,128]{2,1,0:T(8,128)S(1)}, f32[40,16,128]{2,1,0:T(8,128)S(1)}, u32[]{:S(2)}, u32[]{:S(2)}) collective-permute-start(f32[40,16,128]{2,1,0:T(8,128)S(1)} %get-tuple-element.30), channel_id=1, source_target_pairs={{0,31},{1,0},{2,1},{3,2},{4,3},{5,4},{6,5},{7,6},{8,7},{9,8},{10,9... | collective-permute-start | bytes 983048 | tf_op jit(solution)/shard_map/ppermute | solution.py:22
  10.6 94.7 %collective-permute-start.1 = (f32[40,16,128]{2,1,0:T(8,128)S(1)}, f32[40,16,128]{2,1,0:T(8,128)S(1)}, u32[]{:S(2)}, u32[]{:S(2)}) collective-permute-start(f32[40,16,128]{2,1,0:T(8,128)S(1)} %get-tuple-element.31), channel_id=1, source_target_pairs={{0,2},{1,3},{2,4},{3,5},{4,6},{5,7},{6,8},{7,9},{8,10},{9,11},{10,... | collective-permute-start | bytes 983048 | tf_op jit(solution)/shard_map/ppermute | solution.py:22
  11.5 93.8 %collective-permute-start = (f32[40,16,128]{2,1,0:T(8,128)S(1)}, f32[40,16,128]{2,1,0:T(8,128)S(1)}, u32[]{:S(2)}, u32[]{:S(2)}) collective-permute-start(f32[40,16,128]{2,1,0:T(8,128)S(1)} %get-tuple-element.31), channel_id=1, source_target_pairs={{0,1},{1,2},{2,3},{3,4},{4,5},{5,6},{6,7},{7,8},{8,9},{9,10},{10,1... | collective-permute-start | bytes 983048 | tf_op jit(solution)/shard_map/ppermute | solution.py:22
  50.4 1.3 copy-start.16
  105.3 0.7 copy-start.10
  105.3 0.8 copy-start.11
  105.3 0.9 copy-start.12
  105.3 1.0 copy-start.13
  239.3 4.1 %copy-start.1 = (f32[1024,128]{1,0:T(8,128)S(1)}, f32[1024,128]{1,0:T(8,128)}, u32[]{:S(2)}) copy-start(f32[1024,128]{1,0:T(8,128)} %get-tuple-element.11) | copy-start | bytes 1572868
  239.3 4.9 %copy-start.2 = (f32[2,64,128]{2,1,0:T(8,128)S(1)}, f32[2,64,128]{2,1,0:T(8,128)}, u32[]{:S(2)}) copy-start(f32[2,64,128]{2,1,0:T(8,128)} %get-tuple-element.12) | copy-start | bytes 196612
Sparse Core Ops, SparseCore 0:
  47.0 30.4 all-reduce.2

commit v3 on v2

--- a/solution.py
+++ b/solution.py
@@ -331,13 +331,6 @@
     chunk = bus_rows // areas
     zt = jnp.transpose(transfer_impedance, (0, 2, 1)).reshape(2 * members, bus_rows)
     zc = jnp.transpose(zt.reshape(2 * members, areas, chunk), (1, 0, 2))
-    all_bus = lax.all_gather(port_bus, "area", axis=0, tiled=False).reshape(-1)
-    local = all_bus - lax.axis_index("row") * bus_rows
-    pick = (jnp.arange(bus_rows, dtype=jnp.int32)[:, None] == local[None, :]).astype(F32)
-    picked = jnp.dot(zt, pick, precision=lax.Precision.HIGHEST).reshape(2 * members, areas, group, ports)
-    picked = lax.psum_scatter(picked, "row", scatter_dimension=2, tiled=True).reshape(2 * members, areas * ports)
-    picked = lax.all_gather(picked, "area", axis=0, tiled=True)
-    zport = lax.dynamic_slice_in_dim(picked, lax.axis_index("area") * ports, ports, 1)
 
     pad = 128 - lines - convs - ports
     index = jnp.concatenate([line_node, conv_node, port_node, jnp.full((1, pad), -1, jnp.int32)], axis=1)
@@ -353,7 +346,7 @@
     angles = jnp.arange(1, STEPS + 1, dtype=F32) * jnp.float32(2.0 * math.pi / STEPS)
     trig = jnp.stack([jnp.cos(angles), jnp.sin(angles)])
     flops = 2 * STEPS * (nodes + 128) * (2 * nodes + 256) * 256
-    waves, hist_end, conv_out, flat, bus_voltage = pl.pallas_call(
+    waves, hist_end, conv_out, _, bus_voltage = pl.pallas_call(
         functools.partial(window_kernel, lines, convs, ports),
         out_shape=(
             jax.ShapeDtypeStruct((STEPS, lines, cases), F32),
@@ -412,8 +405,14 @@
         zc,
     )
 
-    seen = lax.dot_general(zport, flat, (((0,), (0,)), ((), ())), precision=lax.Precision.HIGHEST)
-    port_voltage = jnp.stack([seen[:, :cases], seen[:, cases:]])[:, None]
+    local = port_bus.reshape(-1) - lax.axis_index("row") * bus_rows
+    inside = (local >= 0) & (local < bus_rows)
+    local = jnp.clip(local, 0, bus_rows - 1)
+    chosen = jnp.concatenate([local, local + bus_rows])
+    taken = jnp.take(bus_voltage.reshape(2 * bus_rows, cases), chosen, axis=0, mode="clip")
+    taken = jnp.where(jnp.concatenate([inside, inside])[:, None], taken, 0.0)
+    taken = taken.reshape(2, port_bus.shape[0], port_bus.shape[1], cases)
+    port_voltage = lax.psum_scatter(taken, "row", scatter_dimension=1, tiled=True)
     return (waves[None], hist_end[None], conv_out[None], bus_voltage, port_voltage)
 
 

time: 257 us -> 181 us (0.70)
  blocking collectives: 58.5 us -> 11.4 us
  between operations: 14.9 us -> 1.42 us
  waiting for transfers between devices: 25.3 us -> 12.4 us
  Pallas kernels: 133 us -> 126 us
  local copies, waits for them, and re-layouts: 15.1 us -> 20 us
  matrix products: 3.8 us -> 0 us
    all_gather x2 -> x0, blocking collectives: 58.5 us -> none  [the longest x1 32.2 us: per_device(): all_bus = lax.all_gather(port_bus, 'area', axis=0, tiled=False).reshape(-1)]
    unnamed x2 -> x0, waiting for transfers between devices: 25.3 us -> none
    ppermute x4, waiting for transfers between devices: 0.01 us -> 12.4 us  [shifted(): return lax.ppermute(x, axes, [(i, (i + by) % size) for i in range(size)])]
    unnamed x0 -> x1, blocking collectives: none -> 11.4 us
    pallas_call x1, Pallas kernels: 133 us -> 126 us  [per_device(): pl.pallas_call(functools.partial(window_kernel, lines, convs, ports), out...]
    unnamed x40 -> x31, local copies, waits for them, and re-layouts: 10.2 us -> 14.4 us
    dot_general x2 -> x0, matrix products: 3.8 us -> none  [the longest x1 2.05 us: per_device(): jnp.dot(zt, pick, precision=lax.Precision.HIGHEST)]
    gather x0 -> x1, local copies, waits for them, and re-layouts: none -> 3.08 us  [per_device(): jnp.take(bus_voltage.reshape(2 * bus_rows, cases), chosen, axis=0, mode='...]
  transfers between devices with their start and end apart: 5 -> 4, of which waited for: 1 -> 3; matrix products, arithmetic and copies ran while one was open for 3% -> 5% of each run, Pallas kernels for 0% -> 0%
where the time goes in v3:
time: 181 us; the launch traced here: 179 us
  Pallas kernels  126 us (70%)
  local copies, waits for them, and re-layouts  20 us (11%)
  waiting for transfers between devices  12.4 us (7%)
  blocking collectives  11.4 us (6%)
  other arithmetic  4.63 us (3%)
  starting transfers between devices  3.21 us (2%)
    pallas_call x1, Pallas kernels, per_device(): pl.pallas_call(functools.partial(window_kernel, lines, convs, ports), out...  126 us
    unnamed x31, local copies, waits for them, and re-layouts  14.4 us
    ppermute x4, waiting for transfers between devices, shifted(): return lax.ppermute(x, axes, [(i, (i + by) % size) for i in range(size)])  12.4 us
    unnamed x1, blocking collectives  11.4 us
  transfers between devices with their start and end apart: 4, of which 3 were waited for; matrix products, arithmetic and copies ran while one was open for 5% of the time, Pallas kernels for 0%

profile of v3, /device:TPU:20, one launch (start us, length us, event | category | flops | bytes accessed | tf_op | source)
XLA Modules:
  0.0 178.9 jit_solution(17011591792037738066)
XLA Ops:
  0.6 0.0 copy-start.11
  0.6 0.0 copy-start.5
  0.7 0.0 copy-start.3
  0.7 0.0 copy-start.4
  0.7 0.0 copy-start
  0.7 0.0 copy-start.1
  0.7 0.0 copy-start.2
  0.7 0.0 copy-start.10
  0.7 1.2 fusion.3
  1.9 0.6 collective-permute-start.3
  2.4 1.5 collective-permute-start.2
  3.9 0.9 collective-permute-start.1
  4.9 0.2 collective-permute-start
  5.2 0.7 and_bitcast_fusion
  5.8 0.7 subtract_clamp_fusion
  7.2 0.7 broadcast_multiply_fusion
  7.8 0.1 min.12
  7.9 0.1 pad_add_fusion.1
  8.0 1.6 copy.28
  9.6 1.3 copy.30
  10.9 0.0 copy-done.11
  10.9 0.6 dynamic-slice
  11.5 0.6 pad_maximum_fusion.trig_ref
  12.1 0.0 copy-done.5
  12.1 0.0 copy-done.3
  12.1 0.0 copy-done.4
  12.1 0.7 maximum_maximum_fusion.coef_ref
  12.8 0.0 copy-done
  12.8 0.0 copy-done.1
  12.8 0.0 copy-done.2
  12.8 0.6 bitcast_add_fusion.index_ref
  13.4 0.0 copy-done.10
  13.4 0.5 and_select_fusion.reach_ref
  13.9 6.0 %collective-permute-done.3.above2_ref = f32[40,16,128]{2,1,0:T(8,128)S(1)} collective-permute-done((f32[40,16,128]{2,1,0:T(8,128)S(1)}, f32[40,16,128]{2,1,0:T(8,128)S(1)}, u32[]{:S(2)}, u32[]{:S(2)}) %collective-permute-start.3) | collective-permute-done | bytes 327712 | tf_op jit(solution)/shard_map/ppermute | solution.py:22
  20.0 0.0 copy-start.6
  20.0 3.5 %collective-permute-done.2.above1_ref = f32[40,16,128]{2,1,0:T(8,128)S(1)} collective-permute-done((f32[40,16,128]{2,1,0:T(8,128)S(1)}, f32[40,16,128]{2,1,0:T(8,128)S(1)}, u32[]{:S(2)}, u32[]{:S(2)}) %collective-permute-start.2) | collective-permute-done | bytes 327712 | tf_op jit(solution)/shard_map/ppermute | solution.py:22
  23.5 0.0 copy-start.7
  23.5 0.0 collective-permute-done.1.below2_ref
  23.5 0.0 copy-start.8
  23.5 2.9 %collective-permute-done.below1_ref = f32[40,16,128]{2,1,0:T(8,128)S(1)} collective-permute-done((f32[40,16,128]{2,1,0:T(8,128)S(1)}, f32[40,16,128]{2,1,0:T(8,128)S(1)}, u32[]{:S(2)}, u32[]{:S(2)}) %collective-permute-start) | collective-permute-done | bytes 327712 | tf_op jit(solution)/shard_map/ppermute | solution.py:22
  26.3 0.0 copy-start.9
  26.3 0.0 copy-done.6
  26.3 0.0 copy-done.7
  26.3 0.0 copy-done.8
  26.3 0.7 copy-done.9
  27.1 125.8 %window.1 = (f32[20,32,128]{2,1,0:T(8,128)}, f32[1024,128]{1,0:T(8,128)}, f32[2,64,128]{2,1,0:T(8,128)}, f32[512,256]{1,0:T(8,128)}, f32[2,5120,128]{2,1,0:T(8,128)}) custom-call(s32[32]{0:T(128)} %and_select_fusion.reach_ref, s32[32]{0:T(128)} %bitcast.42, f32[2,20]{1,0:T(2,128)} %pad_maximum_fusion.trig_ref, s32[1]{0:T(128)S(6)} %copy.35.count_ref, ...), custom_call_target="tpu_custom_call" | custom-call | flops 27179089920 | bytes 8000000 | tf_op jit(solution)/shard_map/window/pallas_call | solution.py:349
  152.9 3.1 %gather_fusion = f32[64,128]{1,0:T(8,128)S(1)} fusion(f32[10240,128]{1,0:T(8,128)} %bitcast.28, s32[1024]{0:T(1024)S(1)} %pad_clamp_fusion), kind=kCustom, calls=%fused_computation | custom fusion | bytes 65792 | tf_op jit(solution)/shard_map/jit(_take)/gather | solution.py:412
  156.0 0.1 broadcast_select_fusion
  156.1 11.4 %all-reduce = f32[2,4,8,128]{3,2,1,0:T(8,128)S(1)} all-reduce(f32[2,4,8,128]{3,2,1,0:T(8,128)S(1)} %broadcast_select_fusion), channel_id=2, replica_groups=mesh['area'=8,'row'=4] {'row'}, use_global_device_ids=true, to_apply=%region_0.1.clone | all-reduce | flops 8192 | bytes 65536
  167.5 1.2 constant_dynamic-slice_fusion
  168.7 1.7 copy.36
  170.4 1.9 %copy.37 = f32[1,1024,128]{2,1,0:T(8,128)} copy(f32[1,1024,128]{2,1,0:T(8,128)} %bitcast.33) | data formatting | bytes 1048576
  172.3 1.5 copy.38
  173.8 5.2 %copy.39 = f32[2,5120,128]{2,1,0:T(8,128)} copy(f32[2,5120,128]{2,1,0:T(8,128)} %get-tuple-element.25) | data formatting | bytes 10485760
  (8 shorter events, 0.1 us)
Async XLA Ops:
  0.6 10.2 %copy-start.11 = (u32[32]{0:T(128)S(1)}, u32[32]{0:T(128)}, u32[]{:S(2)}) copy-start(u32[32]{0:T(128)} %constant.66) | copy-start | bytes 388
  0.6 11.4 %copy-start.5 = (f32[1,8]{1,0:T(1,128)S(1)}, f32[1,8]{1,0:T(1,128)}, u32[]{:S(2)}) copy-start(f32[1,8]{1,0:T(1,128)} %param.34) | copy-start | bytes 100
  0.7 11.4 %copy-start.3 = (f32[1,64]{1,0:T(1,128)S(1)}, f32[1,64]{1,0:T(1,128)}, u32[]{:S(2)}) copy-start(f32[1,64]{1,0:T(1,128)} %param.32) | copy-start | bytes 772
  0.7 11.4 %copy-start.4 = (f32[1,64]{1,0:T(1,128)S(1)}, f32[1,64]{1,0:T(1,128)}, u32[]{:S(2)}) copy-start(f32[1,64]{1,0:T(1,128)} %param.31) | copy-start | bytes 772
  0.7 12.1 %copy-start = (s32[1,8]{1,0:T(1,128)S(1)}, s32[1,8]{1,0:T(1,128)}, u32[]{:S(2)}) copy-start(s32[1,8]{1,0:T(1,128)} %param.33) | copy-start | bytes 100
  0.7 12.1 %copy-start.1 = (s32[1,64]{1,0:T(1,128)S(1)}, s32[1,64]{1,0:T(1,128)}, u32[]{:S(2)}) copy-start(s32[1,64]{1,0:T(1,128)} %param.27) | copy-start | bytes 772
  0.7 12.1 %copy-start.2 = (s32[1,32]{1,0:T(1,128)S(1)}, s32[1,32]{1,0:T(1,128)}, u32[]{:S(2)}) copy-start(s32[1,32]{1,0:T(1,128)} %param.24) | copy-start | bytes 388
  0.7 12.7 %copy-start.10 = (s32[1,32]{1,0:T(1,128)S(1)}, s32[1,32]{1,0:T(1,128)}, u32[]{:S(2)}) copy-start(s32[1,32]{1,0:T(1,128)} %param.23) | copy-start | bytes 388
  1.9 18.1 %collective-permute-start.3 = (f32[40,16,128]{2,1,0:T(8,128)S(1)}, f32[40,16,128]{2,1,0:T(8,128)S(1)}, u32[]{:S(2)}, u32[]{:S(2)}) collective-permute-start(f32[40,16,128]{2,1,0:T(8,128)S(1)} %get-tuple-element.13), channel_id=1, source_target_pairs={{0,30},{1,31},{2,0},{3,1},{4,2},{5,3},{6,4},{7,5},{8,6},{9,7},{10,... | collective-permute-start | bytes 983048 | tf_op jit(solution)/shard_map/ppermute | solution.py:22
  2.4 21.0 %collective-permute-start.2 = (f32[40,16,128]{2,1,0:T(8,128)S(1)}, f32[40,16,128]{2,1,0:T(8,128)S(1)}, u32[]{:S(2)}, u32[]{:S(2)}) collective-permute-start(f32[40,16,128]{2,1,0:T(8,128)S(1)} %get-tuple-element.13), channel_id=1, source_target_pairs={{0,31},{1,0},{2,1},{3,2},{4,3},{5,4},{6,5},{7,6},{8,7},{9,8},{10,9... | collective-permute-start | bytes 983048 | tf_op jit(solution)/shard_map/ppermute | solution.py:22
  3.9 19.5 %collective-permute-start.1 = (f32[40,16,128]{2,1,0:T(8,128)S(1)}, f32[40,16,128]{2,1,0:T(8,128)S(1)}, u32[]{:S(2)}, u32[]{:S(2)}) collective-permute-start(f32[40,16,128]{2,1,0:T(8,128)S(1)} %get-tuple-element.14), channel_id=1, source_target_pairs={{0,2},{1,3},{2,4},{3,5},{4,6},{5,7},{6,8},{7,9},{8,10},{9,11},{10,... | collective-permute-start | bytes 983048 | tf_op jit(solution)/shard_map/ppermute | solution.py:22
  4.9 21.5 %collective-permute-start = (f32[40,16,128]{2,1,0:T(8,128)S(1)}, f32[40,16,128]{2,1,0:T(8,128)S(1)}, u32[]{:S(2)}, u32[]{:S(2)}) collective-permute-start(f32[40,16,128]{2,1,0:T(8,128)S(1)} %get-tuple-element.14), channel_id=1, source_target_pairs={{0,1},{1,2},{2,3},{3,4},{4,5},{5,6},{6,7},{7,8},{8,9},{9,10},{10,1... | collective-permute-start | bytes 983048 | tf_op jit(solution)/shard_map/ppermute | solution.py:22
  20.0 6.4 %copy-start.6 = (f32[40,16,128]{2,1,0:T(8,128)}, f32[40,16,128]{2,1,0:T(8,128)S(1)}, u32[]{:S(2)}) copy-start(f32[40,16,128]{2,1,0:T(8,128)S(1)} %collective-permute-done.3.above2_ref) | copy-start | bytes 983044
  23.5 2.9 %copy-start.7 = (f32[40,16,128]{2,1,0:T(8,128)}, f32[40,16,128]{2,1,0:T(8,128)S(1)}, u32[]{:S(2)}) copy-start(f32[40,16,128]{2,1,0:T(8,128)S(1)} %collective-permute-done.2.above1_ref) | copy-start | bytes 983044
  23.5 2.9 %copy-start.8 = (f32[40,16,128]{2,1,0:T(8,128)}, f32[40,16,128]{2,1,0:T(8,128)S(1)}, u32[]{:S(2)}) copy-start(f32[40,16,128]{2,1,0:T(8,128)S(1)} %collective-permute-done.1.below2_ref) | copy-start | bytes 983044
  26.3 0.7 copy-start.9
